TPU v7x, 512 devices: a whole 4x8x8 slice. The times are simulated.
512 devices in a mesh: gx: 32 (over z, x), gy: 16 (over y, core).
Axes of the slice: x: 4, y: 8, z: 8, core: 2. Of those that a mesh axis runs over, the one named last changes fastest.
Arguments:
- velocity_guess: float32 [8, 2, 1024, 4096], P(None, None, 'gx', 'gy'), may hold values from -6 to 6
- friction: bfloat16 [8, 1024, 4096], P(None, 'gx', 'gy'), may hold values from 0.5 to 4
- thickness: float32 [1024, 4096], P('gx', 'gy'), may hold values from 0.5 to 4.5
- surface: float32 [1024, 4096], P('gx', 'gy'), may hold values from -4 to 1284
- ice_mask: int32 [1024, 4096], P('gx', 'gy'), may hold values 0 or 1
- grounded_mask: int32 [1024, 4096], P('gx', 'gy'), may hold values 0 or 1
Outputs:
- velocity: float32 [8, 2, 1024, 4096], P(None, None, 'gx', 'gy')
All inputs are finite; a program needn't handle non-finite values. No bound on the sum of `ice_mask` or of `grounded_mask` on one device may be relied on, other than what follows from the above.
Results may differ from a plain program's by a relative error of at most 0.0003.
Values sent between devices are 32-bit elements; how exact they have to be, the bound alone decides.
A program may use at most 64 MiB of HBM per device.

v0:
```python
import jax
import jax.numpy as jnp
from jax import lax
from jax.sharding import PartitionSpec as P

strain_floor = 0.1
water_drag = 0.25
flow_power = 1.0 / 3.0


def padded_2(cells, sides, width):
    for axis, dim in sides:
        count = lax.axis_size(axis)
        ends = count - 1
        head = lax.slice_in_dim(cells, 0, width, axis=dim)
        tail = lax.slice_in_dim(cells, cells.shape[dim] - width, cells.shape[dim], axis=dim)
        cells = jnp.concatenate(
            [
                lax.ppermute(tail, axis, [(i, (i + 1) % count) for i in range(ends)]),
                cells,
                lax.ppermute(head, axis, [((i + 1) % count, i) for i in range(ends)]),
            ],
            axis=dim,
        )
    return cells


def centre_rows(padded):
    return 0.5 * (padded[..., 2:, 1:-1] - padded[..., :-2, 1:-1])


def centre_cols(padded):
    return 0.5 * (padded[..., 1:-1, 2:] - padded[..., 1:-1, :-2])


def strains(padded):
    field_u = padded[:, 0]
    field_v = padded[:, 1]
    return (centre_rows(field_u), centre_cols(field_v), centre_cols(field_u) + centre_rows(field_v))


def stresses(visc, padded):
    ka, kb, kc = strains(padded)
    return (visc * (4.0 * ka + 2.0 * kb), visc * (2.0 * ka + 4.0 * kb), visc * kc)


def divergence(sxx, syy, sxy, field, drag, icef):
    out_u = icef * (drag * field[:, 0] - centre_rows(sxx) - centre_cols(sxy))
    out_v = icef * (drag * field[:, 1] - centre_cols(syy) - centre_rows(sxy))
    return jnp.stack([out_u, out_v], 1)


def extend(field):
    flat = field.reshape((-1,) + field.shape[2:])
    grown = padded_2(flat, (("gx", 1), ("gy", 2)), 1)
    return grown.reshape(field.shape[:2] + grown.shape[1:])


def member_dot(left, right):
    return lax.psum(jnp.sum(left * right, axis=(1, 2, 3)), ("gx", "gy"))


def column(values):
    return values[:, None, None, None]


def per_device(velocity_guess, friction, thickness, surface, ice_mask, grounded_mask):
    members = velocity_guess.shape[0]
    icef = ice_mask.astype(jnp.float32)
    groundf = grounded_mask.astype(jnp.float32)
    drag = icef * (groundf * friction.astype(jnp.float32) + water_drag)
    start = icef * velocity_guess
    stacked = jnp.concatenate([start.reshape((-1,) + start.shape[2:]), surface[None]], 0)
    grown = padded_2(stacked, (("gx", 1), ("gy", 2)), 1)
    start_ext = grown[: 2 * members].reshape((members, 2) + grown.shape[1:])
    start_one = grown[: 2 * members].reshape((members, 2) + grown.shape[1:])
    surf_one = grown[2 * members]
    sa, sb, sc = strains(start_one)
    visc = (
        icef
        * 0.5
        * thickness
        * jnp.power(sa * sa + sb * sb + sa * sb + 0.25 * (sc * sc) + strain_floor, -flow_power)
    )
    visc_ext = padded_2(visc, (("gx", 1), ("gy", 2)), 1)
    near_rows = visc_ext[:, 2:, 1:-1] + visc_ext[:, :-2, 1:-1]
    near_cols = visc_ext[:, 1:-1, 2:] + visc_ext[:, 1:-1, :-2]
    precond = jnp.stack(
        [
            icef * (near_rows + 0.25 * near_cols + drag) + (1.0 - icef),
            icef * (near_cols + 0.25 * near_rows + drag) + (1.0 - icef),
        ],
        1,
    )
    force = jnp.stack(
        [icef * -(thickness * centre_rows(surf_one)), icef * -(thickness * centre_cols(surf_one))],
        0,
    )

    def operate(padded):
        sxx, syy, sxy = stresses(visc, padded)
        joined = jnp.concatenate([sxx, syy, sxy], 0)
        wider = padded_2(joined, (("gx", 1), ("gy", 2)), 1)
        field = padded[:, :, 1:-1, 1:-1]
        return divergence(
            wider[:members], wider[members : 2 * members], wider[2 * members :], field, drag, icef
        )

    velocity = start
    resid = force[None] - operate(start_ext)
    scaled = resid / precond
    direction = scaled
    norm_now = member_dot(resid, scaled)
    for step in range(2):
        image = operate(extend(direction))
        alpha = norm_now / member_dot(direction, image)
        velocity = velocity + column(alpha) * direction
        resid = resid - column(alpha) * image
        if step == 0:
            scaled = resid / precond
            norm_next = member_dot(resid, scaled)
            direction = scaled + column(norm_next / norm_now) * direction
            norm_now = norm_next
    return velocity


def solution(mesh):
    placed = (
        P(None, None, "gx", "gy"),
        P(None, "gx", "gy"),
        P("gx", "gy"),
        P("gx", "gy"),
        P("gx", "gy"),
        P("gx", "gy"),
    )
    return jax.shard_map(
        per_device, mesh=mesh, in_specs=placed, out_specs=P(None, None, "gx", "gy"), check_vma=False
    )
```

profile of v0, /device:TPU:1, one launch (start us, length us, event | category | flops | bytes accessed | tf_op | source)
XLA Modules:
  0.0 479.3 jit_solution(5027223697449381866)
XLA Ops:
  1.9 3.9 collective-permute-start
  7.2 3.2 collective-permute-done.1
  10.6 5.2 %collective-permute-start.2 = (f32[17,34,1]{2,1,0:T(8,128)S(1)}, f32[17,34,1]{2,1,0:T(8,128)S(1)}, u32[]{:S(2)}, u32[]{:S(2)}) collective-permute-start(f32[17,34,1]{2,1,0:T(8,128)S(1)} %get-tuple-element.39), channel_id=1, source_target_pairs={{0,1},{1,2},{2,3},{3,4},{4,5},{5,6},{6,7},{7,8},{8,9},{9,10},{10,1... | collective-permute-start | bytes 6944 | tf_op jit(solution)/shard_map/ppermute | solution.py:19
  15.8 3.4 collective-permute-start.3
  20.0 4.4 collective-permute-done.3
  28.3 4.0 collective-permute-start.9
  33.6 4.0 collective-permute-start.5
  37.8 2.1 collective-permute-start.10
  39.9 3.6 collective-permute-start.11
  48.7 4.4 collective-permute-start.7
  53.2 4.5 collective-permute-done.6
  59.8 5.3 %collective-permute-start.12 = (f32[16,1,256]{2,1,0:T(1,128)S(1)}, f32[16,1,256]{2,1,0:T(1,128)S(1)}, u32[]{:S(2)}, u32[]{:S(2)}) collective-permute-start(f32[16,1,256]{2,1,0:T(1,128)S(1)} %get-tuple-element.50), channel_id=1, source_target_pairs={{0,16},{16,32},{32,48},{48,64},{64,80},{80,96},{96,112},{112,128},... | collective-permute-start | bytes 49160 | tf_op jit(solution)/shard_map/ppermute | solution.py:19
  66.4 5.3 %collective-permute-done.13 = f32[16,1,256]{2,1,0:T(1,128)S(1)} collective-permute-done((f32[16,1,256]{2,1,0:T(1,128)S(1)}, f32[16,1,256]{2,1,0:T(1,128)S(1)}, u32[]{:S(2)}, u32[]{:S(2)}) %collective-permute-start.13) | collective-permute-done | bytes 16416 | tf_op jit(solution)/shard_map/ppermute | solution.py:21
  71.9 5.5 %collective-permute-start.14 = (f32[16,34,1]{2,1,0:T(8,128)S(1)}, f32[16,34,1]{2,1,0:T(8,128)S(1)}, u32[]{:S(2)}, u32[]{:S(2)}) collective-permute-start(f32[16,34,1]{2,1,0:T(8,128)S(1)} %get-tuple-element.43), channel_id=1, source_target_pairs={{0,1},{1,2},{2,3},{3,4},{4,5},{5,6},{6,7},{7,8},{8,9},{9,10},{10,1... | collective-permute-start | bytes 6536 | tf_op jit(solution)/shard_map/ppermute | solution.py:19
  77.5 1.9 collective-permute-start.15
  79.4 2.1 collective-permute-done.14
  81.5 4.4 collective-permute-done.15
  88.3 6.1 %collective-permute-start.17 = (f32[24,1,256]{2,1,0:T(1,128)S(1)}, f32[24,1,256]{2,1,0:T(1,128)S(1)}, u32[]{:S(2)}, u32[]{:S(2)}) collective-permute-start(f32[24,1,256]{2,1,0:T(1,128)S(1)} %get-tuple-element.36), channel_id=1, source_target_pairs={{0,16},{16,32},{32,48},{48,64},{64,80},{80,96},{96,112},{112,128},... | collective-permute-start | bytes 73736 | tf_op jit(solution)/shard_map/ppermute | solution.py:19
  97.6 3.6 collective-permute-start.19
  101.3 4.6 collective-permute-done.18
  108.8 120.4 %all-reduce = (f32[8]{0:T(128)S(1)}, f32[8]{0:T(128)S(1)}) all-reduce(f32[8]{0:T(128)S(1)} %get-tuple-element.6, f32[8]{0:T(128)S(1)} %get-tuple-element.5), channel_id=1, replica_groups=mesh['gx'=32,'gy'=16] {'gx','gy'}, use_global_device_ids=true, to_apply=%region_1.0 | all-reduce | flops 16 | bytes 128 | tf_op jit(solution)/shard_map/psum | solution.py:60
  229.2 2.2 fusion.63
  231.6 95.5 %psum.30 = f32[8]{0:T(128)S(1)} all-reduce(f32[8]{0:T(128)S(1)} %get-tuple-element.13), channel_id=1, replica_groups=mesh['gx'=32,'gy'=16] {'gx','gy'}, use_global_device_ids=true, to_apply=%region_5.0 | all-reduce | flops 8 | bytes 64 | tf_op jit(solution)/shard_map/psum | solution.py:60
  329.1 2.8 collective-permute-start.20
  333.3 3.2 collective-permute-done.21
  336.7 5.9 %collective-permute-start.22 = (f32[16,34,1]{2,1,0:T(8,128)S(1)}, f32[16,34,1]{2,1,0:T(8,128)S(1)}, u32[]{:S(2)}, u32[]{:S(2)}) collective-permute-start(f32[16,34,1]{2,1,0:T(8,128)S(1)} %get-tuple-element.41), channel_id=1, source_target_pairs={{0,1},{1,2},{2,3},{3,4},{4,5},{5,6},{6,7},{7,8},{8,9},{9,10},{10,1... | collective-permute-start | bytes 6536 | tf_op jit(solution)/shard_map/ppermute | solution.py:19
  342.6 2.1 collective-permute-start.23
  346.6 4.4 collective-permute-done.23
  353.5 4.0 collective-permute-start.25
  360.7 3.6 collective-permute-start.27
  364.3 4.6 collective-permute-done.26
  371.6 106.7 %psum.31 = f32[8]{0:T(128)S(1)} all-reduce(f32[8]{0:T(128)S(1)} %fusion), channel_id=1, replica_groups=mesh['gx'=32,'gy'=16] {'gx','gy'}, use_global_device_ids=true, to_apply=%region_7.0 | all-reduce | flops 8 | bytes 64 | tf_op jit(solution)/shard_map/psum | solution.py:60
  (124 shorter events, 41.8 us)
Async XLA Ops:
  0.8 106.6 %copy-start.1 = (f32[32,256]{1,0:T(8,128)}, f32[32,256]{1,0:T(8,128)S(1)}, u32[]{:S(2)}) copy-start(f32[32,256]{1,0:T(8,128)S(1)} %convert_element_type.9) | copy-start | bytes 98308
  1.9 5.3 %collective-permute-start = (f32[17,1,256]{2,1,0:T(1,128)S(1)}, f32[17,1,256]{2,1,0:T(1,128)S(1)}, u32[]{:S(2)}, u32[]{:S(2)}) collective-permute-start(f32[17,1,256]{2,1,0:T(1,128)S(1)} %get-tuple-element.45), channel_id=1, source_target_pairs={{0,16},{16,32},{32,48},{48,64},{64,80},{80,96},{96,112},{112,128},... | collective-permute-start | bytes 52232 | tf_op jit(solution)/shard_map/ppermute | solution.py:19
  5.9 4.5 collective-permute-start.1
  10.6 9.4 %collective-permute-start.2 = (f32[17,34,1]{2,1,0:T(8,128)S(1)}, f32[17,34,1]{2,1,0:T(8,128)S(1)}, u32[]{:S(2)}, u32[]{:S(2)}) collective-permute-start(f32[17,34,1]{2,1,0:T(8,128)S(1)} %get-tuple-element.39), channel_id=1, source_target_pairs={{0,1},{1,2},{2,3},{3,4},{4,5},{5,6},{6,7},{7,8},{8,9},{9,10},{10,1... | collective-permute-start | bytes 6944 | tf_op jit(solution)/shard_map/ppermute | solution.py:19
  15.8 8.6 %collective-permute-start.3 = (f32[17,34,1]{2,1,0:T(8,128)S(1)}, f32[17,34,1]{2,1,0:T(8,128)S(1)}, u32[]{:S(2)}, u32[]{:S(2)}) collective-permute-start(f32[17,34,1]{2,1,0:T(8,128)S(1)} %get-tuple-element.40), channel_id=1, source_target_pairs={{1,0},{2,1},{3,2},{4,3},{5,4},{6,5},{7,6},{8,7},{9,8},{10,9},{11,1... | collective-permute-start | bytes 6944 | tf_op jit(solution)/shard_map/ppermute | solution.py:21
  27.0 10.6 %collective-permute-start.8 = (f32[8,1,256]{2,1,0:T(1,128)S(1)}, f32[8,1,256]{2,1,0:T(1,128)S(1)}, u32[]{:S(2)}, u32[]{:S(2)}) collective-permute-start(f32[8,1,256]{2,1,0:T(1,128)S(1)} %get-tuple-element.56), channel_id=1, source_target_pairs={{16,0},{32,16},{48,32},{64,48},{80,64},{96,80},{112,96},{128,112},... | collective-permute-start | bytes 24584 | tf_op jit(solution)/shard_map/ppermute | solution.py:21
  28.3 9.3 %collective-permute-start.9 = (f32[8,1,256]{2,1,0:T(1,128)S(1)}, f32[8,1,256]{2,1,0:T(1,128)S(1)}, u32[]{:S(2)}, u32[]{:S(2)}) collective-permute-start(f32[8,1,256]{2,1,0:T(1,128)S(1)} %get-tuple-element.57), channel_id=1, source_target_pairs={{0,16},{16,32},{32,48},{48,64},{64,80},{80,96},{96,112},{112,128},... | collective-permute-start | bytes 24584 | tf_op jit(solution)/shard_map/ppermute | solution.py:19
  32.3 14.1 %collective-permute-start.4 = (f32[24,1,256]{2,1,0:T(1,128)S(1)}, f32[24,1,256]{2,1,0:T(1,128)S(1)}, u32[]{:S(2)}, u32[]{:S(2)}) collective-permute-start(f32[24,1,256]{2,1,0:T(1,128)S(1)} %get-tuple-element.37), channel_id=1, source_target_pairs={{16,0},{32,16},{48,32},{64,48},{80,64},{96,80},{112,96},{128,112},... | collective-permute-start | bytes 73736 | tf_op jit(solution)/shard_map/ppermute | solution.py:21
  33.6 12.8 %collective-permute-start.5 = (f32[24,1,256]{2,1,0:T(1,128)S(1)}, f32[24,1,256]{2,1,0:T(1,128)S(1)}, u32[]{:S(2)}, u32[]{:S(2)}) collective-permute-start(f32[24,1,256]{2,1,0:T(1,128)S(1)} %get-tuple-element.38), channel_id=1, source_target_pairs={{0,16},{16,32},{32,48},{48,64},{64,80},{80,96},{96,112},{112,128},... | collective-permute-start | bytes 73736 | tf_op jit(solution)/shard_map/ppermute | solution.py:19
  37.8 6.8 %collective-permute-start.10 = (f32[8,34,1]{2,1,0:T(8,128)S(1)}, f32[8,34,1]{2,1,0:T(8,128)S(1)}, u32[]{:S(2)}, u32[]{:S(2)}) collective-permute-start(f32[8,34,1]{2,1,0:T(8,128)S(1)} %get-tuple-element.52), channel_id=1, source_target_pairs={{1,0},{2,1},{3,2},{4,3},{5,4},{6,5},{7,6},{8,7},{9,8},{10,9},{11,1... | collective-permute-start | bytes 3272 | tf_op jit(solution)/shard_map/ppermute | solution.py:21
  39.9 5.9 %collective-permute-start.11 = (f32[8,34,1]{2,1,0:T(8,128)S(1)}, f32[8,34,1]{2,1,0:T(8,128)S(1)}, u32[]{:S(2)}, u32[]{:S(2)}) collective-permute-start(f32[8,34,1]{2,1,0:T(8,128)S(1)} %get-tuple-element.53), channel_id=1, source_target_pairs={{0,1},{1,2},{2,3},{3,4},{4,5},{5,6},{6,7},{7,8},{8,9},{9,10},{10,1... | collective-permute-start | bytes 3272 | tf_op jit(solution)/shard_map/ppermute | solution.py:19
  46.8 10.9 %collective-permute-start.6 = (f32[24,34,1]{2,1,0:T(8,128)S(1)}, f32[24,34,1]{2,1,0:T(8,128)S(1)}, u32[]{:S(2)}, u32[]{:S(2)}) collective-permute-start(f32[24,34,1]{2,1,0:T(8,128)S(1)} %get-tuple-element.29), channel_id=1, source_target_pairs={{1,0},{2,1},{3,2},{4,3},{5,4},{6,5},{7,6},{8,7},{9,8},{10,9},{11,1... | collective-permute-start | bytes 9800 | tf_op jit(solution)/shard_map/ppermute | solution.py:21
  48.7 10.1 %collective-permute-start.7 = (f32[24,34,1]{2,1,0:T(8,128)S(1)}, f32[24,34,1]{2,1,0:T(8,128)S(1)}, u32[]{:S(2)}, u32[]{:S(2)}) collective-permute-start(f32[24,34,1]{2,1,0:T(8,128)S(1)} %get-tuple-element.30), channel_id=1, source_target_pairs={{0,1},{1,2},{2,3},{3,4},{4,5},{5,6},{6,7},{7,8},{8,9},{9,10},{10,1... | collective-permute-start | bytes 9800 | tf_op jit(solution)/shard_map/ppermute | solution.py:19
  59.8 6.6 %collective-permute-start.12 = (f32[16,1,256]{2,1,0:T(1,128)S(1)}, f32[16,1,256]{2,1,0:T(1,128)S(1)}, u32[]{:S(2)}, u32[]{:S(2)}) collective-permute-start(f32[16,1,256]{2,1,0:T(1,128)S(1)} %get-tuple-element.50), channel_id=1, source_target_pairs={{0,16},{16,32},{32,48},{48,64},{64,80},{80,96},{96,112},{112,128},... | collective-permute-start | bytes 49160 | tf_op jit(solution)/shard_map/ppermute | solution.py:19
  65.1 6.6 %collective-permute-start.13 = (f32[16,1,256]{2,1,0:T(1,128)S(1)}, f32[16,1,256]{2,1,0:T(1,128)S(1)}, u32[]{:S(2)}, u32[]{:S(2)}) collective-permute-start(f32[16,1,256]{2,1,0:T(1,128)S(1)} %get-tuple-element.51), channel_id=1, source_target_pairs={{16,0},{32,16},{48,32},{64,48},{80,64},{96,80},{112,96},{128,112},... | collective-permute-start | bytes 49160 | tf_op jit(solution)/shard_map/ppermute | solution.py:21
  71.9 9.5 %collective-permute-start.14 = (f32[16,34,1]{2,1,0:T(8,128)S(1)}, f32[16,34,1]{2,1,0:T(8,128)S(1)}, u32[]{:S(2)}, u32[]{:S(2)}) collective-permute-start(f32[16,34,1]{2,1,0:T(8,128)S(1)} %get-tuple-element.43), channel_id=1, source_target_pairs={{0,1},{1,2},{2,3},{3,4},{4,5},{5,6},{6,7},{7,8},{8,9},{9,10},{10,1... | collective-permute-start | bytes 6536 | tf_op jit(solution)/shard_map/ppermute | solution.py:19
  77.5 8.4 %collective-permute-start.15 = (f32[16,34,1]{2,1,0:T(8,128)S(1)}, f32[16,34,1]{2,1,0:T(8,128)S(1)}, u32[]{:S(2)}, u32[]{:S(2)}) collective-permute-start(f32[16,34,1]{2,1,0:T(8,128)S(1)} %get-tuple-element.44), channel_id=1, source_target_pairs={{1,0},{2,1},{3,2},{4,3},{5,4},{6,5},{7,6},{8,7},{9,8},{10,9},{11,1... | collective-permute-start | bytes 6536 | tf_op jit(solution)/shard_map/ppermute | solution.py:21
  87.0 7.4 %collective-permute-start.16 = (f32[24,1,256]{2,1,0:T(1,128)S(1)}, f32[24,1,256]{2,1,0:T(1,128)S(1)}, u32[]{:S(2)}, u32[]{:S(2)}) collective-permute-start(f32[24,1,256]{2,1,0:T(1,128)S(1)} %get-tuple-element.35), channel_id=1, source_target_pairs={{16,0},{32,16},{48,32},{64,48},{80,64},{96,80},{112,96},{128,112},... | collective-permute-start | bytes 73736 | tf_op jit(solution)/shard_map/ppermute | solution.py:21
  88.3 7.0 %collective-permute-start.17 = (f32[24,1,256]{2,1,0:T(1,128)S(1)}, f32[24,1,256]{2,1,0:T(1,128)S(1)}, u32[]{:S(2)}, u32[]{:S(2)}) collective-permute-start(f32[24,1,256]{2,1,0:T(1,128)S(1)} %get-tuple-element.36), channel_id=1, source_target_pairs={{0,16},{16,32},{32,48},{48,64},{64,80},{80,96},{96,112},{112,128},... | collective-permute-start | bytes 73736 | tf_op jit(solution)/shard_map/ppermute | solution.py:19
  95.7 10.1 %collective-permute-start.18 = (f32[24,34,1]{2,1,0:T(8,128)S(1)}, f32[24,34,1]{2,1,0:T(8,128)S(1)}, u32[]{:S(2)}, u32[]{:S(2)}) collective-permute-start(f32[24,34,1]{2,1,0:T(8,128)S(1)} %get-tuple-element.25), channel_id=1, source_target_pairs={{1,0},{2,1},{3,2},{4,3},{5,4},{6,5},{7,6},{8,7},{9,8},{10,9},{11,1... | collective-permute-start | bytes 9800 | tf_op jit(solution)/shard_map/ppermute | solution.py:21
  97.6 9.4 %collective-permute-start.19 = (f32[24,34,1]{2,1,0:T(8,128)S(1)}, f32[24,34,1]{2,1,0:T(8,128)S(1)}, u32[]{:S(2)}, u32[]{:S(2)}) collective-permute-start(f32[24,34,1]{2,1,0:T(8,128)S(1)} %get-tuple-element.26), channel_id=1, source_target_pairs={{0,1},{1,2},{2,3},{3,4},{4,5},{5,6},{6,7},{7,8},{8,9},{9,10},{10,1... | collective-permute-start | bytes 9800 | tf_op jit(solution)/shard_map/ppermute | solution.py:19
  329.1 4.1 collective-permute-start.20
  332.0 4.5 collective-permute-start.21
  336.7 9.9 %collective-permute-start.22 = (f32[16,34,1]{2,1,0:T(8,128)S(1)}, f32[16,34,1]{2,1,0:T(8,128)S(1)}, u32[]{:S(2)}, u32[]{:S(2)}) collective-permute-start(f32[16,34,1]{2,1,0:T(8,128)S(1)} %get-tuple-element.41), channel_id=1, source_target_pairs={{0,1},{1,2},{2,3},{3,4},{4,5},{5,6},{6,7},{7,8},{8,9},{9,10},{10,1... | collective-permute-start | bytes 6536 | tf_op jit(solution)/shard_map/ppermute | solution.py:19
  342.6 8.4 %collective-permute-start.23 = (f32[16,34,1]{2,1,0:T(8,128)S(1)}, f32[16,34,1]{2,1,0:T(8,128)S(1)}, u32[]{:S(2)}, u32[]{:S(2)}) collective-permute-start(f32[16,34,1]{2,1,0:T(8,128)S(1)} %get-tuple-element.42), channel_id=1, source_target_pairs={{1,0},{2,1},{3,2},{4,3},{5,4},{6,5},{7,6},{8,7},{9,8},{10,9},{11,1... | collective-permute-start | bytes 6536 | tf_op jit(solution)/shard_map/ppermute | solution.py:21
  352.2 5.3 %collective-permute-start.24 = (f32[24,1,256]{2,1,0:T(1,128)S(1)}, f32[24,1,256]{2,1,0:T(1,128)S(1)}, u32[]{:S(2)}, u32[]{:S(2)}) collective-permute-start(f32[24,1,256]{2,1,0:T(1,128)S(1)} %get-tuple-element.33), channel_id=1, source_target_pairs={{16,0},{32,16},{48,32},{64,48},{80,64},{96,80},{112,96},{128,112},... | collective-permute-start | bytes 73736 | tf_op jit(solution)/shard_map/ppermute | solution.py:21
  353.5 4.9 %collective-permute-start.25 = (f32[24,1,256]{2,1,0:T(1,128)S(1)}, f32[24,1,256]{2,1,0:T(1,128)S(1)}, u32[]{:S(2)}, u32[]{:S(2)}) collective-permute-start(f32[24,1,256]{2,1,0:T(1,128)S(1)} %get-tuple-element.34), channel_id=1, source_target_pairs={{0,16},{16,32},{32,48},{48,64},{64,80},{80,96},{96,112},{112,128},... | collective-permute-start | bytes 73736 | tf_op jit(solution)/shard_map/ppermute | solution.py:19
  358.8 10.1 %collective-permute-start.26 = (f32[24,34,1]{2,1,0:T(8,128)S(1)}, f32[24,34,1]{2,1,0:T(8,128)S(1)}, u32[]{:S(2)}, u32[]{:S(2)}) collective-permute-start(f32[24,34,1]{2,1,0:T(8,128)S(1)} %get-tuple-element.21), channel_id=1, source_target_pairs={{1,0},{2,1},{3,2},{4,3},{5,4},{6,5},{7,6},{8,7},{9,8},{10,9},{11,1... | collective-permute-start | bytes 9800 | tf_op jit(solution)/shard_map/ppermute | solution.py:21
  360.7 9.4 %collective-permute-start.27 = (f32[24,34,1]{2,1,0:T(8,128)S(1)}, f32[24,34,1]{2,1,0:T(8,128)S(1)}, u32[]{:S(2)}, u32[]{:S(2)}) collective-permute-start(f32[24,34,1]{2,1,0:T(8,128)S(1)} %get-tuple-element.22), channel_id=1, source_target_pairs={{0,1},{1,2},{2,3},{3,4},{4,5},{5,6},{6,7},{7,8},{8,9},{9,10},{10,1... | collective-permute-start | bytes 9800 | tf_op jit(solution)/shard_map/ppermute | solution.py:19
  371.3 107.0 %copy-start.9 = (f32[8,2,32,256]{3,2,1,0:T(8,128)S(1)}, f32[8,2,32,256]{3,2,1,0:T(8,128)}, u32[]{:S(2)}) copy-start(f32[8,2,32,256]{3,2,1,0:T(8,128)} %param.6) | copy-start | bytes 1572868
  371.3 107.0 %copy-start.10 = (f32[8,2,32,256]{3,2,0,1:T(8,128)S(1)}, f32[8,2,32,256]{3,2,0,1:T(8,128)}, u32[]{:S(2)}) copy-start(f32[8,2,32,256]{3,2,0,1:T(8,128)} %get-tuple-element.20) | copy-start | bytes 1572868
  371.6 106.7 %copy-start.16 = (f32[8]{0:T(128)S(1)}, f32[8]{0:T(128)}, u32[]{:S(2)}) copy-start(f32[8]{0:T(128)} %copy-done.15) | copy-start | bytes 100
  (13 other events, 197.7 us)
where the time goes:
time: 481 us; the launch traced here: 479 us
  blocking collectives  323 us (67%)
  starting transfers between devices  86.3 us (18%)
  waiting for transfers between devices  50.8 us (11%)
  other arithmetic  13.5 us (3%)
  local copies, waits for them, and re-layouts  5.37 us (1%)
    psum x3, blocking collectives, member_dot(): return lax.psum(jnp.sum(left * right, axis=(1, 2, 3)), ('gx', 'gy'))  323 us
    ppermute x14, starting transfers between devices, padded_2(): lax.ppermute(tail, axis, [(i, (i + 1) % count) for i in range(ends)])  62 us
    ppermute x14, waiting for transfers between devices, padded_2(): lax.ppermute(head, axis, [((i + 1) % count, i) for i in range(ends)])  39.5 us
    ppermute x14, starting transfers between devices, padded_2(): lax.ppermute(head, axis, [((i + 1) % count, i) for i in range(ends)])  24.3 us
    ppermute x14, waiting for transfers between devices, padded_2(): lax.ppermute(tail, axis, [(i, (i + 1) % count) for i in range(ends)])  11.3 us
  transfers between devices with their start and end apart: 28, of which 19 were waited for; matrix products, arithmetic and copies ran while one was open for 0% of the time, Pallas kernels for 0%

commit v1 on v0

v1 whole, which is shorter than its diff:
```python
import jax
import jax.numpy as jnp
from jax import lax
from jax.experimental import pallas as pl
from jax.experimental.pallas import tpu as pltpu
from jax.sharding import PartitionSpec as P

MESH = pl.DeviceIdType.MESH
F32 = jnp.float32

strain_floor = 0.1
water_drag = 0.25
flow_power = 1.0 / 3.0

GUESS_W, DRAG_W, FLAT_W = 5, 3, 4
MEMBER_LANES = 2 * (GUESS_W + GUESS_W + DRAG_W)
U_AT, V_AT, DRAG_AT = GUESS_W, 3 * GUESS_W, 4 * GUESS_W + DRAG_W
PER_TILE = 4
FLAT_AT = PER_TILE * MEMBER_LANES + FLAT_W
EDGE = 8
LANES = 128


def neighbours():
    rows, cols = lax.axis_size("gx"), lax.axis_size("gy")
    me_x, me_y = lax.axis_index("gx"), lax.axis_index("gy")
    up, down = lax.rem(me_x + rows - 1, rows), lax.rem(me_x + 1, rows)
    left, right = lax.rem(me_y + cols - 1, cols), lax.rem(me_y + 1, cols)
    return me_x, me_y, up, down, left, right


def shift(cells, by, axis):
    return pltpu.roll(cells, by % cells.shape[axis], axis)


def diff(cells, axis):
    return shift(cells, -1, axis) - shift(cells, 1, axis)


def near(cells, axis):
    return shift(cells, -1, axis) + shift(cells, 1, axis)


def row_places(members):
    guess = [GUESS_W * i for i in range(2 * members)]
    drag = [GUESS_W * 2 * members + DRAG_W * i for i in range(members)]
    flat = GUESS_W * 2 * members + DRAG_W * members
    return guess, drag, (flat, flat + FLAT_W), flat + 2 * FLAT_W


def halo_kernel(guess_ref, fric_ref, thick_ref, surf_ref, ice_ref, ground_ref,
                from_up, from_down, from_left, from_right,
                go_up, go_down, go_left, go_right, in_up, in_down, in_left, in_right, send_sem, recv_sem):
    me_x, me_y, up, down, left, right = neighbours()
    around = [(up, me_y), (down, me_y), (me_x, left), (me_x, right),
              (up, left), (up, right), (down, left), (down, right)]
    barrier = pltpu.get_barrier_semaphore()
    for place in around:
        pl.semaphore_signal(barrier, inc=1, device_id=place, device_id_type=MESH)

    members, _, rows, cols = guess_ref.shape
    ice = ice_ref[...].astype(F32)
    ground = ground_ref[...].astype(F32)
    thick = ice * thick_ref[...]
    surf = surf_ref[...]
    go_left[...] = jnp.zeros_like(go_left)
    go_right[...] = jnp.zeros_like(go_right)
    guess_at, drag_at, flat_at, _ = row_places(members)
    lane = lax.broadcasted_iota(jnp.int32, (rows, LANES), 1)

    def pack_cols(tile, cells, at, width):
        head = shift(cells[:, :LANES], at, 1)
        tail = shift(cells[:, cols - LANES:], at, 1)
        go_left[tile] = jnp.where((lane >= at) & (lane < at + width), head, go_left[tile])
        go_right[tile] = jnp.where((lane >= at - width) & (lane < at), tail, go_right[tile])

    def pack_rows(cells, at, width):
        go_up[at:at + width, :] = cells[:width, :]
        go_down[at:at + width, :] = cells[rows - width:, :]

    for m in range(members):
        tile, base = m // PER_TILE, (m % PER_TILE) * MEMBER_LANES
        u, v = ice * guess_ref[m, 0], ice * guess_ref[m, 1]
        drag = ice * (ground * fric_ref[m].astype(F32) + water_drag)
        pack_rows(u, guess_at[2 * m], GUESS_W)
        pack_rows(v, guess_at[2 * m + 1], GUESS_W)
        pack_rows(drag, drag_at[m], DRAG_W)
        pack_cols(tile, u, base + U_AT, GUESS_W)
        pack_cols(tile, v, base + V_AT, GUESS_W)
        pack_cols(tile, drag, base + DRAG_AT, DRAG_W)
    pack_rows(thick, flat_at[0], FLAT_W)
    pack_rows(surf, flat_at[1], FLAT_W)
    pack_cols(0, thick, FLAT_AT, FLAT_W)
    pack_cols(1, surf, FLAT_AT, FLAT_W)

    pl.semaphore_wait(barrier, len(around))
    top, mid, low = pl.ds(0, EDGE), pl.ds(EDGE, rows), pl.ds(EDGE + rows, EDGE)
    first, final = pl.ds(0, EDGE), pl.ds(rows - EDGE, EDGE)
    moves = [
        (go_up, in_down),
        (go_down, in_up),
        (go_left, in_right.at[:, mid]),
        (go_right, in_left.at[:, mid]),
        (go_left.at[:, first], in_right.at[:, low]),
        (go_right.at[:, first], in_left.at[:, low]),
        (go_left.at[:, final], in_right.at[:, top]),
        (go_right.at[:, final], in_left.at[:, top]),
    ]
    copies = [
        pltpu.make_async_remote_copy(
            src_ref=source, dst_ref=target, send_sem=send_sem.at[i], recv_sem=recv_sem.at[i],
            device_id=around[i], device_id_type=MESH)
        for i, (source, target) in enumerate(moves)
    ]
    for copy in copies:
        copy.start()
    for copy in copies:
        copy.wait()
    from_up[...] = in_up[...]
    from_down[...] = in_down[...]
    from_left[...] = in_left[...]
    from_right[...] = in_right[...]


def solve_kernel(guess_ref, fric_ref, thick_ref, surf_ref, ice_ref, ground_ref,
                 from_up, from_down, from_left, from_right,
                 z_ref, y_ref, sums_ref,
                 guess_ext, drag_ext, thick_ext, surf_ext, strip):
    members, _, rows, cols = guess_ref.shape
    me_x, me_y = lax.axis_index("gx"), lax.axis_index("gy")
    is_top, is_low = me_x == 0, me_x == lax.axis_size("gx") - 1
    is_left, is_right = me_y == 0, me_y == lax.axis_size("gy") - 1
    guess_at, drag_at, flat_at, _ = row_places(members)
    high = rows + 2 * EDGE

    row = lax.broadcasted_iota(jnp.int32, (high, LANES), 0)
    outside = (is_top & (row < EDGE)) | (is_low & (row >= EDGE + rows))
    for tile in range(2):
        left = jnp.where(is_left, 0.0, from_left[tile])
        right = jnp.where(is_right, 0.0, from_right[tile])
        strip[tile] = jnp.where(outside, 0.0, left + right)

    ice = ice_ref[...].astype(F32)
    ground = ground_ref[...].astype(F32)

    def fill(ext, cells, at, width, tile, lane_at):
        ext[EDGE:EDGE + rows, :cols] = cells
        ext[EDGE - width:EDGE, :cols] = jnp.where(is_top, 0.0, from_up[at:at + width, :])
        ext[EDGE + rows:EDGE + rows + width, :cols] = jnp.where(is_low, 0.0, from_down[at:at + width, :])
        ext[:, cols:] = shift(strip[tile], -lane_at, 1)

    for m in range(members):
        tile, base = m // PER_TILE, (m % PER_TILE) * MEMBER_LANES
        fill(guess_ext.at[m, 0], ice * guess_ref[m, 0], guess_at[2 * m], GUESS_W, tile, base + U_AT)
        fill(guess_ext.at[m, 1], ice * guess_ref[m, 1], guess_at[2 * m + 1], GUESS_W, tile, base + V_AT)
        drag = ice * (ground * fric_ref[m].astype(F32) + water_drag)
        fill(drag_ext.at[m], drag, drag_at[m], DRAG_W, tile, base + DRAG_AT)
    fill(thick_ext, ice * thick_ref[...], flat_at[0], FLAT_W, 0, FLAT_AT)
    fill(surf_ext, surf_ref[...], flat_at[1], FLAT_W, 1, FLAT_AT)

    def member(m, carry):
        thick = thick_ext[...]
        surf = surf_ext[...]
        on_ice = thick > 0.0
        half = 0.5 * thick
        u, v, drag = guess_ext[m, 0], guess_ext[m, 1], drag_ext[m]

        def strains(pu, pv):
            return diff(pu, 0), diff(pv, 1), diff(pu, 1) + diff(pv, 0)

        def form(a, b, c):
            return a * a + b * b + a * b + 0.25 * (c * c)

        def operate(nu_half, pu, pv, a, b, c):
            sxx = nu_half * (2.0 * a + b)
            syy = nu_half * (a + 2.0 * b)
            sxy = nu_half * (0.5 * c)
            return (drag * pu - diff(sxx, 0) - diff(sxy, 1),
                    drag * pv - diff(syy, 1) - diff(sxy, 0))

        a, b, c = strains(u, v)
        nu = half * jnp.exp(-flow_power * jnp.log(0.25 * form(a, b, c) + strain_floor))
        nu_half = 0.5 * nu
        near_rows, near_cols = near(nu, 0), near(nu, 1)
        inv_u = jnp.where(on_ice, 1.0 / (near_rows + 0.25 * near_cols + drag), 0.0)
        inv_v = jnp.where(on_ice, 1.0 / (near_cols + 0.25 * near_rows + drag), 0.0)
        image_u, image_v = operate(nu_half, u, v, a, b, c)
        res_u = -(half * diff(surf, 0)) - image_u
        res_v = -(half * diff(surf, 1)) - image_v
        z_u, z_v = res_u * inv_u, res_v * inv_v
        a, b, c = strains(z_u, z_v)
        image_u, image_v = operate(nu_half, z_u, z_v, a, b, c)
        gap_u, gap_v = image_u - res_u, image_v - res_v
        y_u, y_v = gap_u * inv_u, gap_v * inv_v
        a, b, c = strains(y_u, y_v)
        energy = nu * form(a, b, c) + drag * (y_u * y_u + y_v * y_v)

        def own(cells):
            return cells[EDGE:EDGE + rows, :cols]

        z_ref[m, 0] = own(z_u)
        z_ref[m, 1] = own(z_v)
        y_ref[m, 0] = own(y_u)
        y_ref[m, 1] = own(y_v)
        lane = lax.broadcasted_iota(jnp.int32, (1, LANES), 1)
        line = jnp.zeros((1, LANES), F32)
        for i, cells in enumerate((res_u * z_u + res_v * z_v, res_u * y_u + res_v * y_v,
                                   gap_u * y_u + gap_v * y_v, energy)):
            total = jnp.sum(own(cells), axis=(0, 1), keepdims=True)
            line = jnp.where(lane == i, total, line)
        sums_ref[pl.ds(m, 1), :] = line
        return carry

    lax.fori_loop(0, members, member, 0)


def groups(rows, cols):
    fine = 4 if rows % 4 == 0 else 1
    pair = 2 if cols % 2 == 0 else 1
    me_x, me_y = lax.axis_index("gx"), lax.axis_index("gy")
    deep, wide = me_x // fine, lax.rem(me_x, fine)
    tall, core = me_y // pair, lax.rem(me_y, pair)

    def chips(step):
        rank = lax.rem(wide * pair + core + step, fine * pair)
        return deep * fine + rank // pair, tall * pair + lax.rem(rank, pair)

    def along_y(step):
        return me_x, lax.rem(tall + step, cols // pair) * pair + core

    def along_z(step):
        return lax.rem(deep + step, rows // fine) * fine + wide, me_y

    return [(fine * pair, wide * pair + core, chips), (cols // pair, tall, along_y), (rows // fine, deep, along_z)]


def sum_kernel(sums_ref, out_ref, held, send_sem, recv_sem):
    phases = groups(lax.axis_size("gx"), lax.axis_size("gy"))
    barrier = pltpu.get_barrier_semaphore()
    count = 0
    for size, _, place in phases:
        for step in range(1, size):
            pl.semaphore_signal(barrier, inc=1, device_id=place(step), device_id_type=MESH)
            count += 1
    pl.semaphore_wait(barrier, count)
    total = sums_ref[...]
    for phase, (size, me, place) in enumerate(phases):
        if size == 1:
            continue
        slots = held.at[phase]
        slots[me] = total
        copies = [
            pltpu.make_async_remote_copy(
                src_ref=slots.at[me], dst_ref=slots.at[me], send_sem=send_sem.at[phase, step],
                recv_sem=recv_sem.at[phase, step], device_id=place(step), device_id_type=MESH)
            for step in range(1, size)
        ]
        for copy in copies:
            copy.start()
        for copy in copies:
            copy.wait_recv()
        total = slots[0]
        for i in range(1, size):
            total = total + slots[i]
        for copy in copies:
            copy.wait_send()
    rz, cross, square, energy = (total[:, i:i + 1] for i in range(4))
    scale = rz + cross
    alpha = rz / scale
    mixed = cross + square
    eta = mixed / scale
    top = square - cross * cross / rz
    low = energy - mixed * eta
    step_two = jnp.where(low > 0.0, jnp.maximum(top, 0.0) / low, 0.0)
    lane = lax.broadcasted_iota(jnp.int32, total.shape, 1)
    out_ref[...] = jnp.where(lane == 0, alpha * (1.0 + step_two * eta), -(alpha * step_two))


def per_device(velocity_guess, friction, thickness, surface, ice_mask, grounded_mask):
    members, _, rows, cols = velocity_guess.shape
    fields = (velocity_guess, friction, thickness, surface, ice_mask, grounded_mask)
    packed = row_places(members)[3]
    high = rows + 2 * EDGE
    vmem = pl.BlockSpec(memory_space=pltpu.VMEM)
    line = jax.ShapeDtypeStruct((packed, cols), F32)
    side = jax.ShapeDtypeStruct((2, high, LANES), F32)
    edges = pl.pallas_call(
        halo_kernel,
        out_shape=(line, line, side, side),
        in_specs=[vmem] * 6,
        out_specs=(vmem,) * 4,
        scratch_shapes=[
            pltpu.VMEM((packed, cols), F32), pltpu.VMEM((packed, cols), F32),
            pltpu.VMEM((2, rows, LANES), F32), pltpu.VMEM((2, rows, LANES), F32),
            pltpu.VMEM((packed, cols), F32), pltpu.VMEM((packed, cols), F32),
            pltpu.VMEM((2, high, LANES), F32), pltpu.VMEM((2, high, LANES), F32),
            pltpu.SemaphoreType.DMA((8,)), pltpu.SemaphoreType.DMA((8,)),
        ],
        compiler_params=pltpu.CompilerParams(collective_id=0, has_side_effects=True),
        name="halo",
    )(*fields)
    wide = cols + LANES
    block = jax.ShapeDtypeStruct((members, 2, rows, cols), F32)
    z, y, sums = pl.pallas_call(
        solve_kernel,
        out_shape=(block, block, jax.ShapeDtypeStruct((members, LANES), F32)),
        in_specs=[vmem] * 10,
        out_specs=(vmem,) * 3,
        scratch_shapes=[
            pltpu.VMEM((members, 2, high, wide), F32), pltpu.VMEM((members, high, wide), F32),
            pltpu.VMEM((high, wide), F32), pltpu.VMEM((high, wide), F32),
            pltpu.VMEM((2, high, LANES), F32),
        ],
        compiler_params=pltpu.CompilerParams(vmem_limit_bytes=48 << 20),
        name="solve",
    )(*fields, *edges)
    coefs = pl.pallas_call(
        sum_kernel,
        out_shape=jax.ShapeDtypeStruct((members, LANES), F32),
        in_specs=[vmem],
        out_specs=vmem,
        scratch_shapes=[
            pltpu.VMEM((3, 8, members, LANES), F32),
            pltpu.SemaphoreType.DMA((3, 8)), pltpu.SemaphoreType.DMA((3, 8)),
        ],
        compiler_params=pltpu.CompilerParams(collective_id=1, has_side_effects=True),
        name="sum_all",
    )(sums)
    first, second = coefs[:, 0, None, None, None], coefs[:, 1, None, None, None]
    return ice_mask.astype(F32) * velocity_guess + (first * z + second * y)


def solution(mesh):
    placed = (
        P(None, None, "gx", "gy"),
        P(None, "gx", "gy"),
        P("gx", "gy"),
        P("gx", "gy"),
        P("gx", "gy"),
        P("gx", "gy"),
    )
    return jax.shard_map(
        per_device, mesh=mesh, in_specs=placed, out_specs=P(None, None, "gx", "gy"), check_vma=False
    )
```

time: 481 us -> 54.9 us (0.11)
  blocking collectives: 323 us -> 0 us
  starting transfers between devices: 86.3 us -> 0 us
  waiting for transfers between devices: 50.8 us -> 0 us
  Pallas kernels: 0 us -> 47.6 us
  other arithmetic: 13.5 us -> 1.77 us
    psum x3 -> x0, blocking collectives: 323 us -> none  [member_dot(): return lax.psum(jnp.sum(left * right, axis=(1, 2, 3)), ('gx', 'gy'))]
    ppermute x28 -> x0, starting transfers between devices: 86.3 us -> none  [the longest x14 62 us: padded_2(): lax.ppermute(tail, axis, [(i, (i + 1) % count) for i in range(ends)])]
    ppermute x28 -> x0, waiting for transfers between devices: 50.8 us -> none  [the longest x14 39.5 us: padded_2(): lax.ppermute(head, axis, [((i + 1) % count, i) for i in range(ends)])]
    pallas_call x0 -> x3, Pallas kernels: none -> 47.6 us  [the longest x1 21.2 us: per_device(): pl.pallas_call(halo_kernel, out_shape=(line, line, side, side), in_specs=...]
  transfers between devices with their start and end apart: 28 -> 0, of which waited for: 19 -> 0; matrix products, arithmetic and copies ran while one was open for 0% -> 0% of each run, Pallas kernels for 0% -> 0%
where the time goes in v1:
time: 54.9 us; the launch traced here: 54.5 us
  Pallas kernels  47.6 us (87%)
  local copies, waits for them, and re-layouts  4.97 us (9%)
  other arithmetic  1.77 us (3%)
    pallas_call x1, Pallas kernels, per_device(): pl.pallas_call(halo_kernel, out_shape=(line, line, side, side), in_specs=...  21.2 us
    pallas_call x1, Pallas kernels, per_device(): pl.pallas_call(sum_kernel, out_shape=jax.ShapeDtypeStruct((members, LANES...  19.3 us
    pallas_call x1, Pallas kernels, per_device(): pl.pallas_call(solve_kernel, out_shape=(block, block, jax.ShapeDtypeStruc...  7.15 us
    unnamed x22, local copies, waits for them, and re-layouts  4 us

profile of v1, /device:TPU:1, one launch (start us, length us, event | category | flops | bytes accessed | tf_op | source)
XLA Modules:
  0.0 54.5 jit_solution(8138168178490926722)
XLA Ops:
  0.0 0.0 copy-start
  0.0 0.8 %convert_element_type.3 = f32[32,256]{1,0:T(8,128)S(1)} convert(s32[32,256]{1,0:T(8,128)} %ice_ref.3) | non-fusion elementwise | flops 8192 | bytes 65536 | tf_op jit(solution)/shard_map/convert_element_type | solution.py:330
  0.8 0.0 copy-start.1
  0.8 0.0 copy-start.2
  0.8 0.0 copy-start.3
  0.8 0.0 copy-start.4
  0.8 0.0 copy-start.5
  0.9 21.2 %halo.1 = (f32[112,256]{1,0:T(8,128)}, f32[112,256]{1,0:T(8,128)}, f32[2,48,128]{2,1,0:T(8,128)}, f32[2,48,128]{2,1,0:T(8,128)}) custom-call(f32[8,2,32,256]{3,2,1,0:T(8,128)} %guess_ref.3, bf16[8,32,256]{2,1,0:T(8,128)(2,1)} %fric_ref.3, f32[32,256]{1,0:T(8,128)} %thick_ref.3, f32[32,256]{1,0:T(8,128)} %surf_ref.3, s32[32,256]{1,0:T(8,128)} %ice_ref.3, ...), custom_call_target="tpu_custom_call" | custom-call | tf_op jit(solution)/shard_map/halo/pallas_call | solution.py:287
  22.1 0.0 copy-done
  22.1 0.0 copy-done.1
  22.1 0.0 copy-done.2
  22.1 0.0 copy-done.3
  22.1 0.0 copy-done.4
  22.1 0.0 copy-done.5
  22.1 0.0 copy-start.6
  22.2 0.9 %copy-done.6 = f32[112,256]{1,0:T(8,128)S(1)} copy-done((f32[112,256]{1,0:T(8,128)S(1)}, f32[112,256]{1,0:T(8,128)}, u32[]{:S(2)}) %copy-start.6) | copy-done | bytes 114712
  23.0 0.0 copy-start.7
  23.0 0.9 %copy-done.7 = f32[112,256]{1,0:T(8,128)S(1)} copy-done((f32[112,256]{1,0:T(8,128)S(1)}, f32[112,256]{1,0:T(8,128)}, u32[]{:S(2)}) %copy-start.7) | copy-done | bytes 114712
  23.9 0.0 copy-start.8
  23.9 0.8 %copy-done.8 = f32[2,48,128]{2,1,0:T(8,128)S(1)} copy-done((f32[2,48,128]{2,1,0:T(8,128)S(1)}, f32[2,48,128]{2,1,0:T(8,128)}, u32[]{:S(2)}) %copy-start.8) | copy-done | bytes 49176
  24.7 0.0 copy-start.9
  24.7 0.8 %copy-done.9 = f32[2,48,128]{2,1,0:T(8,128)S(1)} copy-done((f32[2,48,128]{2,1,0:T(8,128)S(1)}, f32[2,48,128]{2,1,0:T(8,128)}, u32[]{:S(2)}) %copy-start.9) | copy-done | bytes 49176
  25.5 7.2 %solve.1 = (f32[8,2,32,256]{3,2,1,0:T(8,128)S(1)}, f32[8,2,32,256]{3,2,1,0:T(8,128)S(1)}, f32[8,128]{1,0:T(8,128)S(1)}) custom-call(f32[8,2,32,256]{3,2,1,0:T(8,128)S(1)} %copy-done, bf16[8,32,256]{2,1,0:T(8,128)(2,1)S(1)} %copy-done.1, f32[32,256]{1,0:T(8,128)S(1)} %copy-done.3, f32[32,256]{1,0:T(8,128)S(1)} %copy-done.4, s32[32,256]{1,0:T(8,128)S(1)} %copy-done.2, ...), custom_call_target="tpu_custom_call" | custom-call | tf_op jit(solution)/shard_map/solve/pallas_call | solution.py:304
  32.7 0.0 copy-start.10
  32.7 0.6 %copy-done.10 = f32[8,128]{1,0:T(8,128)} copy-done((f32[8,128]{1,0:T(8,128)}, f32[8,128]{1,0:T(8,128)S(1)}, u32[]{:S(2)}) %copy-start.10) | copy-done | bytes 4120
  33.3 19.3 %sum_all.1 = f32[8,128]{1,0:T(8,128)} custom-call(f32[8,128]{1,0:T(8,128)} %copy-done.10), custom_call_target="tpu_custom_call" | custom-call | tf_op jit(solution)/shard_map/sum_all/pallas_call | solution.py:317
  52.6 1.0 %slice_reduce_fusion.1 = (f32[8]{0:T(128)S(1)}, f32[8]{0:T(128)S(1)}) fusion(f32[8,128]{1,0:T(8,128)} %sum_all.1), kind=kLoop, calls=%fused_computation.2 | loop fusion | bytes 128 | tf_op jit(solution)/shard_map/slice | solution.py:329
  53.5 1.0 %add_add_fusion = f32[8,2,32,256]{3,2,1,0:T(8,128)} fusion(f32[8,2,32,256]{3,2,1,0:T(8,128)S(1)} %get-tuple-element.18, f32[8,2,32,256]{3,2,1,0:T(8,128)S(1)} %get-tuple-element.17, f32[8,2,32,256]{3,2,1,0:T(8,128)S(1)} %copy-done, f32[8]{0:T(128)S(1)} %get-tuple-element.20, f32[8]{0:T(128)S(1)} %get-tuple-element.19, f32[32,256]{1,0:T(8,128)S(1)} %convert_element_type.3), kind=kLoop, calls=%fused_computation | loop fusion | flops 655360 | bytes 2129984 | tf_op jit(solution)/shard_map/add | solution.py:330
Async XLA Ops:
  0.0 22.1 %copy-start = (f32[8,2,32,256]{3,2,1,0:T(8,128)S(1)}, f32[8,2,32,256]{3,2,1,0:T(8,128)}, u32[]{:S(2)}) copy-start(f32[8,2,32,256]{3,2,1,0:T(8,128)} %guess_ref.3) | copy-start | bytes 1572868
  0.8 21.3 %copy-start.1 = (bf16[8,32,256]{2,1,0:T(8,128)(2,1)S(1)}, bf16[8,32,256]{2,1,0:T(8,128)(2,1)}, u32[]{:S(2)}) copy-start(bf16[8,32,256]{2,1,0:T(8,128)(2,1)} %fric_ref.3) | copy-start | bytes 393220
  0.8 21.3 %copy-start.2 = (s32[32,256]{1,0:T(8,128)S(1)}, s32[32,256]{1,0:T(8,128)}, u32[]{:S(2)}) copy-start(s32[32,256]{1,0:T(8,128)} %ice_ref.3) | copy-start | bytes 98308
  0.8 21.3 %copy-start.3 = (f32[32,256]{1,0:T(8,128)S(1)}, f32[32,256]{1,0:T(8,128)}, u32[]{:S(2)}) copy-start(f32[32,256]{1,0:T(8,128)} %thick_ref.3) | copy-start | bytes 98308
  0.8 21.3 %copy-start.4 = (f32[32,256]{1,0:T(8,128)S(1)}, f32[32,256]{1,0:T(8,128)}, u32[]{:S(2)}) copy-start(f32[32,256]{1,0:T(8,128)} %surf_ref.3) | copy-start | bytes 98308
  0.8 21.3 %copy-start.5 = (s32[32,256]{1,0:T(8,128)S(1)}, s32[32,256]{1,0:T(8,128)}, u32[]{:S(2)}) copy-start(s32[32,256]{1,0:T(8,128)} %ground_ref.3) | copy-start | bytes 98308
  22.1 0.9 %copy-start.6 = (f32[112,256]{1,0:T(8,128)S(1)}, f32[112,256]{1,0:T(8,128)}, u32[]{:S(2)}) copy-start(f32[112,256]{1,0:T(8,128)} %get-tuple-element.12.from_up) | copy-start | bytes 344068
  23.0 0.9 %copy-start.7 = (f32[112,256]{1,0:T(8,128)S(1)}, f32[112,256]{1,0:T(8,128)}, u32[]{:S(2)}) copy-start(f32[112,256]{1,0:T(8,128)} %get-tuple-element.13.from_down) | copy-start | bytes 344068
  23.9 0.8 %copy-start.8 = (f32[2,48,128]{2,1,0:T(8,128)S(1)}, f32[2,48,128]{2,1,0:T(8,128)}, u32[]{:S(2)}) copy-start(f32[2,48,128]{2,1,0:T(8,128)} %get-tuple-element.14.from_left) | copy-start | bytes 147460
  24.7 0.8 %copy-start.9 = (f32[2,48,128]{2,1,0:T(8,128)S(1)}, f32[2,48,128]{2,1,0:T(8,128)}, u32[]{:S(2)}) copy-start(f32[2,48,128]{2,1,0:T(8,128)} %get-tuple-element.15.from_right) | copy-start | bytes 147460
  32.7 0.6 %copy-start.10 = (f32[8,128]{1,0:T(8,128)}, f32[8,128]{1,0:T(8,128)S(1)}, u32[]{:S(2)}) copy-start(f32[8,128]{1,0:T(8,128)S(1)} %get-tuple-element.16.sums_ref) | copy-start | bytes 12292

commit v2 on v1

v2 whole, which is shorter than its diff:
```python
import itertools

import jax
import jax.numpy as jnp
from jax import lax
from jax.experimental import pallas as pl
from jax.experimental.pallas import tpu as pltpu
from jax.sharding import PartitionSpec as P

MESH = pl.DeviceIdType.MESH
F32 = jnp.float32

strain_floor = 0.1
water_drag = 0.25
flow_power = 1.0 / 3.0

GUESS_W, DRAG_W, FLAT_W = 5, 3, 4
MEMBER_LANES = 2 * (GUESS_W + GUESS_W + DRAG_W)
U_AT, V_AT, DRAG_AT = GUESS_W, 3 * GUESS_W, 4 * GUESS_W + DRAG_W
PER_TILE = 4
FLAT_AT = PER_TILE * MEMBER_LANES + FLAT_W
EDGE = 8
LANES = 128
QUARTER = LANES // 4


def neighbours():
    rows, cols = lax.axis_size("gx"), lax.axis_size("gy")
    me_x, me_y = lax.axis_index("gx"), lax.axis_index("gy")
    up, down = lax.rem(me_x + rows - 1, rows), lax.rem(me_x + 1, rows)
    left, right = lax.rem(me_y + cols - 1, cols), lax.rem(me_y + 1, cols)
    return me_x, me_y, up, down, left, right


def shift(cells, by, axis):
    return pltpu.roll(cells, by % cells.shape[axis], axis)


def diff(cells, axis):
    return shift(cells, -1, axis) - shift(cells, 1, axis)


def near(cells, axis):
    return shift(cells, -1, axis) + shift(cells, 1, axis)


def row_places(members):
    guess = [GUESS_W * i for i in range(2 * members)]
    drag = [GUESS_W * 2 * members + DRAG_W * i for i in range(members)]
    flat = GUESS_W * 2 * members + DRAG_W * members
    return guess, drag, (flat, flat + FLAT_W), flat + 2 * FLAT_W


def spread(axes):
    sizes = [size for size, _, _ in axes]
    place = 0
    for size, mine, _ in axes:
        place = place * size + mine
    steps = [step for step in itertools.product(*map(range, sizes)) if any(step)]

    def reach(step):
        return sum(min(by, size - by) * far for by, (size, _, far) in zip(step, axes))

    steps.sort(key=lambda step: -reach(step))
    return place, [[lax.rem(mine + by, size) for by, (size, mine, _) in zip(step, axes)] for step in steps]


def groups():
    rows, cols = lax.axis_size("gx"), lax.axis_size("gy")
    fine = 4 if rows % 4 == 0 else 1
    pair = 2 if cols % 2 == 0 else 1
    me_x, me_y = lax.axis_index("gx"), lax.axis_index("gy")
    place_y, others_y = spread([(cols // pair, me_y // pair, 1.0), (pair, lax.rem(me_y, pair), 0.1)])
    place_x, others_x = spread([(rows // fine, me_x // fine, 1.0), (fine, lax.rem(me_x, fine), 1.0)])
    return [
        (cols, place_y, [(me_x, chip * pair + core) for chip, core in others_y]),
        (rows, place_x, [(deep * fine + wide, me_y) for deep, wide in others_x]),
    ]


def kernel(guess_hbm, fric_hbm, thick_hbm, surf_hbm, ice_hbm, ground_hbm, out_ref,
           guess_ref, fric_ref, thick_ref, surf_ref, ice_ref, ground_ref,
           go_up, go_down, go_left, go_right, in_up, in_down, in_left, in_right,
           guess_ext, drag_ext, thick_ext, surf_ext, strip, z_ref, y_ref, held,
           load_sem, send_sem, recv_sem, push_sem, pull_sem):
    me_x, me_y, up, down, left, right = neighbours()
    around = [(up, me_y), (down, me_y), (me_x, left), (me_x, right),
              (up, left), (up, right), (down, left), (down, right)]
    phases = groups()
    sources = (ice_hbm, ground_hbm, thick_hbm, surf_hbm, guess_hbm, fric_hbm)
    targets = (ice_ref, ground_ref, thick_ref, surf_ref, guess_ref, fric_ref)
    loads = [pltpu.make_async_copy(source, target, load_sem.at[i])
             for i, (source, target) in enumerate(zip(sources, targets))]
    for load in loads:
        load.start()

    barrier = pltpu.get_barrier_semaphore()
    greeted = [place for _, _, others in phases[::-1] for place in others] + around
    for place in greeted:
        pl.semaphore_signal(barrier, inc=1, device_id=place, device_id_type=MESH)

    members, _, rows, cols = guess_ref.shape
    high = rows + 2 * EDGE
    is_top, is_low = me_x == 0, me_x == lax.axis_size("gx") - 1
    is_left, is_right = me_y == 0, me_y == lax.axis_size("gy") - 1
    guess_at, drag_at, flat_at, _ = row_places(members)

    go_left[...] = jnp.zeros_like(go_left)
    go_right[...] = jnp.zeros_like(go_right)
    for load in loads:
        load.wait()
    ice = ice_ref[...].astype(F32)
    ground = ground_ref[...].astype(F32)
    lane = lax.broadcasted_iota(jnp.int32, (rows, LANES), 1)

    def pack(ext, cells, row_at, width, tile, lane_at):
        ext[EDGE:EDGE + rows, :cols] = cells
        go_up[row_at:row_at + width, :] = cells[:width, :]
        go_down[row_at:row_at + width, :] = cells[rows - width:, :]
        head = shift(cells[:, :LANES], lane_at, 1)
        tail = shift(cells[:, cols - LANES:], lane_at, 1)
        go_left[tile] = jnp.where((lane >= lane_at) & (lane < lane_at + width), head, go_left[tile])
        go_right[tile] = jnp.where((lane >= lane_at - width) & (lane < lane_at), tail, go_right[tile])

    def every_field(act):
        for m in range(members):
            tile, base = m // PER_TILE, (m % PER_TILE) * MEMBER_LANES
            act(guess_ext.at[m, 0], lambda: ice * guess_ref[m, 0], guess_at[2 * m], GUESS_W, tile, base + U_AT)
            act(guess_ext.at[m, 1], lambda: ice * guess_ref[m, 1], guess_at[2 * m + 1], GUESS_W, tile, base + V_AT)
            act(drag_ext.at[m], lambda: ice * (ground * fric_ref[m].astype(F32) + water_drag),
                drag_at[m], DRAG_W, tile, base + DRAG_AT)
        act(thick_ext, lambda: ice * thick_ref[...], flat_at[0], FLAT_W, 0, FLAT_AT)
        act(surf_ext, lambda: surf_ref[...], flat_at[1], FLAT_W, 1, FLAT_AT)

    every_field(lambda ext, cells, *where: pack(ext, cells(), *where))

    pl.semaphore_wait(barrier, len(greeted))
    above, mid, below = pl.ds(0, EDGE), pl.ds(EDGE, rows), pl.ds(EDGE + rows, EDGE)
    first, final = pl.ds(0, EDGE), pl.ds(rows - EDGE, EDGE)
    moves = [
        (go_up, in_down),
        (go_down, in_up),
        (go_left, in_right.at[:, mid]),
        (go_right, in_left.at[:, mid]),
        (go_left.at[:, first], in_right.at[:, below]),
        (go_right.at[:, first], in_left.at[:, below]),
        (go_left.at[:, final], in_right.at[:, above]),
        (go_right.at[:, final], in_left.at[:, above]),
    ]
    copies = [
        pltpu.make_async_remote_copy(
            src_ref=source, dst_ref=target, send_sem=send_sem.at[i], recv_sem=recv_sem.at[i],
            device_id=around[i], device_id_type=MESH)
        for i, (source, target) in enumerate(moves)
    ]
    for copy in copies:
        copy.start()
    for copy in copies:
        copy.wait_recv()

    row = lax.broadcasted_iota(jnp.int32, (high, LANES), 0)
    outside = (is_top & (row < EDGE)) | (is_low & (row >= EDGE + rows))
    for tile in range(2):
        west = jnp.where(is_left, 0.0, in_left[tile])
        east = jnp.where(is_right, 0.0, in_right[tile])
        strip[tile] = jnp.where(outside, 0.0, west + east)

    def fill(ext, cells, row_at, width, tile, lane_at):
        ext[EDGE - width:EDGE, :cols] = jnp.where(is_top, 0.0, in_up[row_at:row_at + width, :])
        ext[EDGE + rows:EDGE + rows + width, :cols] = jnp.where(is_low, 0.0, in_down[row_at:row_at + width, :])
        ext[:, cols:] = shift(strip[tile], -lane_at, 1)

    every_field(fill)

    def member(m, line):
        thick = thick_ext[...]
        surf = surf_ext[...]
        on_ice = thick > 0.0
        half = 0.5 * thick
        u, v, drag = guess_ext[m, 0], guess_ext[m, 1], drag_ext[m]

        def strains(pu, pv):
            return diff(pu, 0), diff(pv, 1), diff(pu, 1) + diff(pv, 0)

        def form(a, b, c):
            return a * a + b * b + a * b + 0.25 * (c * c)

        def operate(nu_half, pu, pv, a, b, c):
            sxx = nu_half * (2.0 * a + b)
            syy = nu_half * (a + 2.0 * b)
            sxy = nu_half * (0.5 * c)
            return (drag * pu - diff(sxx, 0) - diff(sxy, 1),
                    drag * pv - diff(syy, 1) - diff(sxy, 0))

        a, b, c = strains(u, v)
        nu = half * jnp.exp(-flow_power * jnp.log(0.25 * form(a, b, c) + strain_floor))
        nu_half = 0.5 * nu
        near_rows, near_cols = near(nu, 0), near(nu, 1)
        inv_u = jnp.where(on_ice, 1.0 / (near_rows + 0.25 * near_cols + drag), 0.0)
        inv_v = jnp.where(on_ice, 1.0 / (near_cols + 0.25 * near_rows + drag), 0.0)
        image_u, image_v = operate(nu_half, u, v, a, b, c)
        res_u = -(half * diff(surf, 0)) - image_u
        res_v = -(half * diff(surf, 1)) - image_v
        z_u, z_v = res_u * inv_u, res_v * inv_v
        a, b, c = strains(z_u, z_v)
        image_u, image_v = operate(nu_half, z_u, z_v, a, b, c)
        gap_u, gap_v = image_u - res_u, image_v - res_v
        y_u, y_v = gap_u * inv_u, gap_v * inv_v
        a, b, c = strains(y_u, y_v)
        energy = nu * form(a, b, c) + drag * (y_u * y_u + y_v * y_v)

        def own(cells):
            return cells[EDGE:EDGE + rows, :cols]

        z_ref[m, 0] = own(z_u)
        z_ref[m, 1] = own(z_v)
        y_ref[m, 0] = own(y_u)
        y_ref[m, 1] = own(y_v)
        slot = lax.broadcasted_iota(jnp.int32, (1, LANES), 1)
        for i, cells in enumerate((res_u * z_u + res_v * z_v, res_u * y_u + res_v * y_v,
                                   gap_u * y_u + gap_v * y_v, energy)):
            total = jnp.sum(own(cells), axis=(0, 1), keepdims=True)
            line = jnp.where(slot == i * QUARTER + m, total, line)
        return line

    total = lax.fori_loop(0, members, member, jnp.zeros((1, LANES), F32))

    pushes = []
    for phase, (size, me, others) in enumerate(phases):
        slots = held.at[phase]
        slots[me] = total
        batch = [
            pltpu.make_async_remote_copy(
                src_ref=slots.at[me], dst_ref=slots.at[me], send_sem=push_sem.at[phase, i],
                recv_sem=pull_sem.at[phase], device_id=place, device_id_type=MESH)
            for i, place in enumerate(others)
        ]
        for push in batch:
            push.start()
        everything = slots.at[pl.ds(0, size - 1)]
        pltpu.make_async_copy(everything, everything, pull_sem.at[phase]).wait()
        total = slots[0]
        for i in range(1, size):
            total = total + slots[i]
        pushes += batch

    rz, cross, square, energy = (shift(total, -i * QUARTER, 1) for i in range(4))
    scale = rz + cross
    alpha = rz / scale
    mixed = cross + square
    eta = mixed / scale
    top = square - cross * cross / rz
    low = energy - mixed * eta
    step_two = jnp.where(low > 0.0, jnp.maximum(top, 0.0) / low, 0.0)
    to_z, to_y = alpha * (1.0 + step_two * eta), -(alpha * step_two)
    for m in range(members):
        by_z, by_y = to_z[:, m:m + 1], to_y[:, m:m + 1]
        for i in range(2):
            out_ref[m, i] = guess_ext[m, i, EDGE:EDGE + rows, :cols] + (by_z * z_ref[m, i] + by_y * y_ref[m, i])
    for copy in copies + pushes:
        copy.wait_send()


def per_device(velocity_guess, friction, thickness, surface, ice_mask, grounded_mask):
    members, _, rows, cols = velocity_guess.shape
    fields = (velocity_guess, friction, thickness, surface, ice_mask, grounded_mask)
    packed = row_places(members)[3]
    high, wide = rows + 2 * EDGE, cols + LANES
    count_x, count_y = lax.axis_size("gx"), lax.axis_size("gy")
    most = max(count_x, count_y)
    line, block, side = (packed, cols), (2, rows, LANES), (2, high, LANES)
    field = (members, 2, rows, cols)
    return pl.pallas_call(
        kernel,
        out_shape=jax.ShapeDtypeStruct(field, F32),
        in_specs=[pl.BlockSpec(memory_space=pltpu.HBM)] * 6,
        out_specs=pl.BlockSpec(memory_space=pltpu.VMEM),
        scratch_shapes=[pltpu.VMEM(array.shape, array.dtype) for array in fields]
        + [pltpu.VMEM(shape, F32) for shape in (
            line, line, block, block, line, line, side, side,
            (members, 2, high, wide), (members, high, wide), (high, wide), (high, wide), side,
            field, field, (2, most, 1, LANES))]
        + [pltpu.SemaphoreType.DMA((6,)), pltpu.SemaphoreType.DMA((8,)), pltpu.SemaphoreType.DMA((8,)),
           pltpu.SemaphoreType.DMA((2, most)), pltpu.SemaphoreType.DMA((2,))],
        compiler_params=pltpu.CompilerParams(
            collective_id=0, has_side_effects=True, vmem_limit_bytes=60 << 20),
        name="ice",
    )(*fields)


def solution(mesh):
    placed = (
        P(None, None, "gx", "gy"),
        P(None, "gx", "gy"),
        P("gx", "gy"),
        P("gx", "gy"),
        P("gx", "gy"),
        P("gx", "gy"),
    )
    return jax.shard_map(
        per_device, mesh=mesh, in_specs=placed, out_specs=P(None, None, "gx", "gy"), check_vma=False
    )
```

time: 54.9 us -> 41.9 us (0.76)
  Pallas kernels: 47.6 us -> 39.9 us
  local copies, waits for them, and re-layouts: 4.97 us -> 1.88 us
  other arithmetic: 1.77 us -> 0 us
    pallas_call x3 -> x1, Pallas kernels: 47.6 us -> 39.9 us  [per_device(): pl.pallas_call(kernel, out_shape=jax.ShapeDtypeStruct(field, F32), in_spe...]
    unnamed x22 -> x1, local copies, waits for them, and re-layouts: 4 us -> 1.88 us
    slice x1 -> x0, local copies, waits for them, and re-layouts: 0.97 us -> none  [per_device(): coefs[:, 0, None, None, None]]
    add x1 -> x0, other arithmetic: 0.95 us -> none  [per_device(): return ice_mask.astype(F32) * velocity_guess + (first * z + second * y)]
    convert_element_type x1 -> x0, other arithmetic: 0.82 us -> none  [per_device(): return ice_mask.astype(F32) * velocity_guess + (first * z + second * y)]
where the time goes in v2:
time: 41.9 us; the launch traced here: 41.8 us
  Pallas kernels  39.9 us (95%)
  local copies, waits for them, and re-layouts  1.88 us (4%)
    pallas_call x1, Pallas kernels, per_device(): pl.pallas_call(kernel, out_shape=jax.ShapeDtypeStruct(field, F32), in_spe...  39.9 us
    unnamed x1, local copies, waits for them, and re-layouts  1.88 us

profile of v2, /device:TPU:1, one launch (start us, length us, event | category | flops | bytes accessed | tf_op | source)
XLA Modules:
  0.0 41.8 jit_solution(8419873038348380605)
XLA Ops:
  0.0 39.9 %ice.1 = f32[8,2,32,256]{3,2,1,0:T(8,128)} custom-call(f32[8,2,32,256]{3,2,1,0:T(8,128)} %guess_hbm.1, bf16[8,32,256]{2,1,0:T(8,128)(2,1)} %fric_hbm.1, f32[32,256]{1,0:T(8,128)} %thick_hbm.1, f32[32,256]{1,0:T(8,128)} %surf_hbm.1, s32[32,256]{1,0:T(8,128)} %ice_hbm.1, s32[32,256]{1,0:T(8,128)} %ground_hbm.1), custom_call_target="tpu_custom_call" | custom-call | tf_op jit(solution)/shard_map/ice/pallas_call | solution.py:273
  39.9 1.9 %copy.8 = f32[8,2,32,256]{3,2,1,0:T(8,128)} copy(f32[8,2,32,256]{3,2,1,0:T(8,128)} %ice.1) | data formatting | bytes 1048576

commit v3 on v2

--- a/solution.py
+++ b/solution.py
@@ -19,8 +19,8 @@
 U_AT, V_AT, DRAG_AT = GUESS_W, 3 * GUESS_W, 4 * GUESS_W + DRAG_W
 PER_TILE = 4
 FLAT_AT = PER_TILE * MEMBER_LANES + FLAT_W
-EDGE = 8
-LANES = 128
+EDGE, HALF = 8, 4
+LANES, TILES = 128, 2
 QUARTER = LANES // 4
 
 
@@ -36,12 +36,22 @@
     return pltpu.roll(cells, by % cells.shape[axis], axis)
 
 
-def diff(cells, axis):
-    return shift(cells, -1, axis) - shift(cells, 1, axis)
-
-
-def near(cells, axis):
-    return shift(cells, -1, axis) + shift(cells, 1, axis)
+def beside(tiles, count):
+    lane = lax.broadcasted_iota(jnp.int32, tiles[0].shape, 1)
+    ahead = [shift(tile, -1, 1) for tile in tiles]
+    behind = [shift(tile, 1, 1) for tile in tiles]
+    ring = len(tiles)
+    after = [jnp.where(lane == LANES - 1, ahead[(t + 1) % ring], ahead[t]) for t in range(count)]
+    before = [jnp.where(lane == 0, behind[t - 1], behind[t]) for t in range(count)]
+    return after, before
+
+
+def diff_cols(tiles, count=3):
+    return [ahead - behind for ahead, behind in zip(*beside(tiles, count))]
+
+
+def form(a, b, c):
+    return a * (a + b) + b * b + c * (0.25 * c)
 
 
 def row_places(members):
@@ -81,7 +91,8 @@
 def kernel(guess_hbm, fric_hbm, thick_hbm, surf_hbm, ice_hbm, ground_hbm, out_ref,
            guess_ref, fric_ref, thick_ref, surf_ref, ice_ref, ground_ref,
            go_up, go_down, go_left, go_right, in_up, in_down, in_left, in_right,
-           guess_ext, drag_ext, thick_ext, surf_ext, strip, z_ref, y_ref, held,
+           guess_ext, drag_ext, thick_ext, surf_ext, strip, z_ref, y_ref,
+           push_u, push_v, nu_ref, sxx_ref, sxy_ref, held,
            load_sem, send_sem, recv_sem, push_sem, pull_sem):
     me_x, me_y, up, down, left, right = neighbours()
     around = [(up, me_y), (down, me_y), (me_x, left), (me_x, right),
@@ -114,7 +125,8 @@
     lane = lax.broadcasted_iota(jnp.int32, (rows, LANES), 1)
 
     def pack(ext, cells, row_at, width, tile, lane_at):
-        ext[EDGE:EDGE + rows, :cols] = cells
+        for t in range(TILES):
+            ext[t, EDGE:EDGE + rows, :] = cells[:, t * LANES:(t + 1) * LANES]
         go_up[row_at:row_at + width, :] = cells[:width, :]
         go_down[row_at:row_at + width, :] = cells[rows - width:, :]
         head = shift(cells[:, :LANES], lane_at, 1)
@@ -166,64 +178,105 @@
         strip[tile] = jnp.where(outside, 0.0, west + east)
 
     def fill(ext, cells, row_at, width, tile, lane_at):
-        ext[EDGE - width:EDGE, :cols] = jnp.where(is_top, 0.0, in_up[row_at:row_at + width, :])
-        ext[EDGE + rows:EDGE + rows + width, :cols] = jnp.where(is_low, 0.0, in_down[row_at:row_at + width, :])
-        ext[:, cols:] = shift(strip[tile], -lane_at, 1)
+        for t in range(TILES):
+            part = slice(t * LANES, (t + 1) * LANES)
+            ext[t, EDGE - width:EDGE, :] = jnp.where(is_top, 0.0, in_up[row_at:row_at + width, part])
+            ext[t, EDGE + rows:EDGE + rows + width, :] = jnp.where(is_low, 0.0, in_down[row_at:row_at + width, part])
+        ext[TILES] = shift(strip[tile], -lane_at, 1)
 
     every_field(fill)
 
+    zero = me_x // lax.axis_size("gx")
+    window, start = rows + 2 * HALF, EDGE - HALF + zero
+
+    def part(ref, tile, by=0):
+        return ref[tile, pl.ds(start + by, window), :]
+
+    def tiles_of(ref, by=0):
+        return [part(ref, t, by) for t in range(TILES + 1)]
+
+    def diff_rows(ref):
+        return [part(ref, t, 1) - part(ref, t, -1) for t in range(TILES + 1)]
+
+    def keep(ref, tiles):
+        for t, tile in enumerate(tiles):
+            ref[t, pl.ds(start, window), :] = tile
+
+    thick = tiles_of(thick_ext)
+    keep(push_u, [0.5 * h * d for h, d in zip(thick, diff_rows(surf_ext))])
+    keep(push_v, [0.5 * h * d for h, d in zip(thick, diff_cols(tiles_of(surf_ext)))])
+
+    def strains(u_ref, v_ref):
+        u, v = tiles_of(u_ref), tiles_of(v_ref)
+        c = [p + q for p, q in zip(diff_cols(u), diff_rows(v_ref))]
+        return u, v, diff_rows(u_ref), diff_cols(v), c
+
+    def operate(nu, drag, u, v, a, b, c):
+        sxx, syy, sxy = [], [], []
+        for n, p, q, w in zip(nu, a, b, c):
+            half, both = 0.5 * n, p + q
+            sxx.append(half * (p + both))
+            syy.append(half * (q + both))
+            sxy.append((0.5 * half) * w)
+        keep(sxx_ref, sxx)
+        keep(sxy_ref, sxy)
+        image_u = [d * p - x - y for d, p, x, y in zip(drag, u, diff_rows(sxx_ref), diff_cols(sxy))]
+        image_v = [d * p - x - y for d, p, x, y in zip(drag, v, diff_cols(syy), diff_rows(sxy_ref))]
+        return image_u, image_v
+
+    own_row = lax.broadcasted_iota(jnp.int32, (window, LANES), 0)
+    own_row = (own_row >= HALF) & (own_row < HALF + rows)
+
     def member(m, line):
-        thick = thick_ext[...]
-        surf = surf_ext[...]
-        on_ice = thick > 0.0
-        half = 0.5 * thick
-        u, v, drag = guess_ext[m, 0], guess_ext[m, 1], drag_ext[m]
-
-        def strains(pu, pv):
-            return diff(pu, 0), diff(pv, 1), diff(pu, 1) + diff(pv, 0)
-
-        def form(a, b, c):
-            return a * a + b * b + a * b + 0.25 * (c * c)
-
-        def operate(nu_half, pu, pv, a, b, c):
-            sxx = nu_half * (2.0 * a + b)
-            syy = nu_half * (a + 2.0 * b)
-            sxy = nu_half * (0.5 * c)
-            return (drag * pu - diff(sxx, 0) - diff(sxy, 1),
-                    drag * pv - diff(syy, 1) - diff(sxy, 0))
-
-        a, b, c = strains(u, v)
-        nu = half * jnp.exp(-flow_power * jnp.log(0.25 * form(a, b, c) + strain_floor))
-        nu_half = 0.5 * nu
-        near_rows, near_cols = near(nu, 0), near(nu, 1)
-        inv_u = jnp.where(on_ice, 1.0 / (near_rows + 0.25 * near_cols + drag), 0.0)
-        inv_v = jnp.where(on_ice, 1.0 / (near_cols + 0.25 * near_rows + drag), 0.0)
-        image_u, image_v = operate(nu_half, u, v, a, b, c)
-        res_u = -(half * diff(surf, 0)) - image_u
-        res_v = -(half * diff(surf, 1)) - image_v
-        z_u, z_v = res_u * inv_u, res_v * inv_v
-        a, b, c = strains(z_u, z_v)
-        image_u, image_v = operate(nu_half, z_u, z_v, a, b, c)
-        gap_u, gap_v = image_u - res_u, image_v - res_v
-        y_u, y_v = gap_u * inv_u, gap_v * inv_v
-        a, b, c = strains(y_u, y_v)
-        energy = nu * form(a, b, c) + drag * (y_u * y_u + y_v * y_v)
-
-        def own(cells):
-            return cells[EDGE:EDGE + rows, :cols]
-
-        z_ref[m, 0] = own(z_u)
-        z_ref[m, 1] = own(z_v)
-        y_ref[m, 0] = own(y_u)
-        y_ref[m, 1] = own(y_v)
+        thick = tiles_of(thick_ext)
+        drag = tiles_of(drag_ext.at[m])
+        u, v, a, b, c = strains(guess_ext.at[m, 0], guess_ext.at[m, 1])
+        nu = [(0.5 * h) * jnp.exp(-flow_power * jnp.log(0.25 * form(p, q, w) + strain_floor))
+              for h, p, q, w in zip(thick, a, b, c)]
+        keep(nu_ref, nu)
+        near_rows = [part(nu_ref, t, 1) + part(nu_ref, t, -1) for t in range(TILES + 1)]
+        near_cols = [ahead + behind for ahead, behind in zip(*beside(nu, TILES + 1))]
+        inv_u = [jnp.where(h > 0.0, 1.0 / (x + 0.25 * y + d), 0.0)
+                 for h, x, y, d in zip(thick, near_rows, near_cols, drag)]
+        inv_v = [jnp.where(h > 0.0, 1.0 / (y + 0.25 * x + d), 0.0)
+                 for h, x, y, d in zip(thick, near_rows, near_cols, drag)]
+        image_u, image_v = operate(nu, drag, u, v, a, b, c)
+        res_u = [-f - q for f, q in zip(tiles_of(push_u), image_u)]
+        res_v = [-f - q for f, q in zip(tiles_of(push_v), image_v)]
+        keep(z_ref.at[m, 0], [r * i for r, i in zip(res_u, inv_u)])
+        keep(z_ref.at[m, 1], [r * i for r, i in zip(res_v, inv_v)])
+        z_u, z_v, a, b, c = strains(z_ref.at[m, 0], z_ref.at[m, 1])
+        image_u, image_v = operate(nu, drag, z_u, z_v, a, b, c)
+        gap_u = [q - r for q, r in zip(image_u, res_u)]
+        gap_v = [q - r for q, r in zip(image_v, res_v)]
+        y_u = [g * i for g, i in zip(gap_u, inv_u)]
+        y_v = [g * i for g, i in zip(gap_v, inv_v)]
+        keep(y_ref.at[m, 0], y_u)
+        keep(y_ref.at[m, 1], y_v)
+
+        def own(ref, tile, by=0):
+            return ref[tile, pl.ds(EDGE + zero + by, rows), :]
+
+        across_u = diff_cols([own(y_ref.at[m, 0], t) for t in range(TILES + 1)], TILES)
+        across_v = diff_cols([own(y_ref.at[m, 1], t) for t in range(TILES + 1)], TILES)
+        energy = []
+        for t in range(TILES):
+            pu, pv = own(y_ref.at[m, 0], t), own(y_ref.at[m, 1], t)
+            a = own(y_ref.at[m, 0], t, 1) - own(y_ref.at[m, 0], t, -1)
+            c = across_u[t] + own(y_ref.at[m, 1], t, 1) - own(y_ref.at[m, 1], t, -1)
+            energy.append(own(nu_ref, t) * form(a, across_v[t], c) + own(drag_ext.at[m], t) * (pu * pu + pv * pv))
+
+        def dot(fu, fv, gu, gv):
+            return [jnp.where(own_row, fu[t] * gu[t] + fv[t] * gv[t], 0.0) for t in range(TILES)]
+
         slot = lax.broadcasted_iota(jnp.int32, (1, LANES), 1)
-        for i, cells in enumerate((res_u * z_u + res_v * z_v, res_u * y_u + res_v * y_v,
-                                   gap_u * y_u + gap_v * y_v, energy)):
-            total = jnp.sum(own(cells), axis=(0, 1), keepdims=True)
+        for i, cells in enumerate((dot(res_u, res_v, z_u, z_v), dot(res_u, res_v, y_u, y_v),
+                                   dot(gap_u, gap_v, y_u, y_v), energy)):
+            total = jnp.sum(sum(cells[1:], cells[0]), axis=(0, 1), keepdims=True)
             line = jnp.where(slot == i * QUARTER + m, total, line)
         return line
 
-    total = lax.fori_loop(0, members, member, jnp.zeros((1, LANES), F32))
+    total = lax.fori_loop(0, members, member, jnp.zeros((1, LANES), F32), unroll=4)
 
     pushes = []
     for phase, (size, me, others) in enumerate(phases):
@@ -256,7 +309,10 @@
     for m in range(members):
         by_z, by_y = to_z[:, m:m + 1], to_y[:, m:m + 1]
         for i in range(2):
-            out_ref[m, i] = guess_ext[m, i, EDGE:EDGE + rows, :cols] + (by_z * z_ref[m, i] + by_y * y_ref[m, i])
+            for t in range(TILES):
+                own = pl.ds(EDGE, rows)
+                out_ref[m, i, :, t * LANES:(t + 1) * LANES] = guess_ext[m, i, t, own, :] + (
+                    by_z * z_ref[m, i, t, own, :] + by_y * y_ref[m, i, t, own, :])
     for copy in copies + pushes:
         copy.wait_send()
 
@@ -265,7 +321,8 @@
     members, _, rows, cols = velocity_guess.shape
     fields = (velocity_guess, friction, thickness, surface, ice_mask, grounded_mask)
     packed = row_places(members)[3]
-    high, wide = rows + 2 * EDGE, cols + LANES
+    high = rows + 2 * EDGE
+    flat = (TILES + 1, high, LANES)
     count_x, count_y = lax.axis_size("gx"), lax.axis_size("gy")
     most = max(count_x, count_y)
     line, block, side = (packed, cols), (2, rows, LANES), (2, high, LANES)
@@ -278,8 +335,8 @@
         scratch_shapes=[pltpu.VMEM(array.shape, array.dtype) for array in fields]
         + [pltpu.VMEM(shape, F32) for shape in (
             line, line, block, block, line, line, side, side,
-            (members, 2, high, wide), (members, high, wide), (high, wide), (high, wide), side,
-            field, field, (2, most, 1, LANES))]
+            (members, 2) + flat, (members,) + flat, flat, flat, side,
+            (members, 2) + flat, (members, 2) + flat, flat, flat, flat, flat, flat, (2, most, 1, LANES))]
         + [pltpu.SemaphoreType.DMA((6,)), pltpu.SemaphoreType.DMA((8,)), pltpu.SemaphoreType.DMA((8,)),
            pltpu.SemaphoreType.DMA((2, most)), pltpu.SemaphoreType.DMA((2,))],
         compiler_params=pltpu.CompilerParams(

time: 41.9 us -> 40.7 us (0.971)
  Pallas kernels: 39.9 us -> 38.7 us
    pallas_call x1, Pallas kernels: 39.9 us -> 38.7 us  [per_device(): pl.pallas_call(kernel, out_shape=jax.ShapeDtypeStruct(field, F32), in_spe...]
where the time goes in v3:
time: 40.7 us; the launch traced here: 40.6 us
  Pallas kernels  38.7 us (95%)
  local copies, waits for them, and re-layouts  1.88 us (5%)
    pallas_call x1, Pallas kernels, per_device(): pl.pallas_call(kernel, out_shape=jax.ShapeDtypeStruct(field, F32), in_spe...  38.7 us
    unnamed x1, local copies, waits for them, and re-layouts  1.88 us

profile of v3, /device:TPU:1, one launch (start us, length us, event | category | flops | bytes accessed | tf_op | source)
XLA Modules:
  0.0 40.6 jit_solution(9679534836773616758)
XLA Ops:
  0.0 38.7 %ice.1 = f32[8,2,32,256]{3,2,1,0:T(8,128)} custom-call(f32[8,2,32,256]{3,2,1,0:T(8,128)} %guess_hbm.1, bf16[8,32,256]{2,1,0:T(8,128)(2,1)} %fric_hbm.1, f32[32,256]{1,0:T(8,128)} %thick_hbm.1, f32[32,256]{1,0:T(8,128)} %surf_hbm.1, s32[32,256]{1,0:T(8,128)} %ice_hbm.1, s32[32,256]{1,0:T(8,128)} %ground_hbm.1), custom_call_target="tpu_custom_call" | custom-call | tf_op jit(solution)/shard_map/ice/pallas_call | solution.py:330
  38.7 1.9 %copy.8 = f32[8,2,32,256]{3,2,1,0:T(8,128)} copy(f32[8,2,32,256]{3,2,1,0:T(8,128)} %ice.1) | data formatting | bytes 1048576

commit v4 on v3

--- a/solution.py
+++ b/solution.py
@@ -21,7 +21,6 @@
 FLAT_AT = PER_TILE * MEMBER_LANES + FLAT_W
 EDGE, HALF = 8, 4
 LANES, TILES = 128, 2
-QUARTER = LANES // 4
 
 
 def neighbours():
@@ -38,11 +37,9 @@
 
 def beside(tiles, count):
     lane = lax.broadcasted_iota(jnp.int32, tiles[0].shape, 1)
-    ahead = [shift(tile, -1, 1) for tile in tiles]
-    behind = [shift(tile, 1, 1) for tile in tiles]
     ring = len(tiles)
-    after = [jnp.where(lane == LANES - 1, ahead[(t + 1) % ring], ahead[t]) for t in range(count)]
-    before = [jnp.where(lane == 0, behind[t - 1], behind[t]) for t in range(count)]
+    after = [shift(jnp.where(lane == 0, tiles[(t + 1) % ring], tiles[t]), -1, 1) for t in range(count)]
+    before = [shift(jnp.where(lane == LANES - 1, tiles[t - 1], tiles[t]), 1, 1) for t in range(count)]
     return after, before
 
 
@@ -54,11 +51,11 @@
     return a * (a + b) + b * b + c * (0.25 * c)
 
 
-def row_places(members):
-    guess = [GUESS_W * i for i in range(2 * members)]
-    drag = [GUESS_W * 2 * members + DRAG_W * i for i in range(members)]
-    flat = GUESS_W * 2 * members + DRAG_W * members
-    return guess, drag, (flat, flat + FLAT_W), flat + 2 * FLAT_W
+def row_places():
+    guess = [GUESS_W * i for i in range(2 * PER_TILE)]
+    drag = [GUESS_W * 2 * PER_TILE + DRAG_W * i for i in range(PER_TILE)]
+    flat = GUESS_W * 2 * PER_TILE + DRAG_W * PER_TILE
+    return guess, drag, (flat, flat + FLAT_W)
 
 
 def spread(axes):
@@ -92,7 +89,7 @@
            guess_ref, fric_ref, thick_ref, surf_ref, ice_ref, ground_ref,
            go_up, go_down, go_left, go_right, in_up, in_down, in_left, in_right,
            guess_ext, drag_ext, thick_ext, surf_ext, strip, z_ref, y_ref,
-           push_u, push_v, nu_ref, sxx_ref, sxy_ref, held,
+           push_u, push_v, nu_ref, sxx_ref, sxy_ref, sums_ref, held,
            load_sem, send_sem, recv_sem, push_sem, pull_sem):
     me_x, me_y, up, down, left, right = neighbours()
     around = [(up, me_y), (down, me_y), (me_x, left), (me_x, right),
@@ -114,7 +111,7 @@
     high = rows + 2 * EDGE
     is_top, is_low = me_x == 0, me_x == lax.axis_size("gx") - 1
     is_left, is_right = me_y == 0, me_y == lax.axis_size("gy") - 1
-    guess_at, drag_at, flat_at, _ = row_places(members)
+    guess_at, drag_at, flat_at = row_places()
 
     go_left[...] = jnp.zeros_like(go_left)
     go_right[...] = jnp.zeros_like(go_right)
@@ -124,50 +121,56 @@
     ground = ground_ref[...].astype(F32)
     lane = lax.broadcasted_iota(jnp.int32, (rows, LANES), 1)
 
-    def pack(ext, cells, row_at, width, tile, lane_at):
+    def pack(ext, cells, row_at, width, group, tile, lane_at):
         for t in range(TILES):
             ext[t, EDGE:EDGE + rows, :] = cells[:, t * LANES:(t + 1) * LANES]
-        go_up[row_at:row_at + width, :] = cells[:width, :]
-        go_down[row_at:row_at + width, :] = cells[rows - width:, :]
+        go_up[group, row_at:row_at + width, :] = cells[:width, :]
+        go_down[group, row_at:row_at + width, :] = cells[rows - width:, :]
         head = shift(cells[:, :LANES], lane_at, 1)
         tail = shift(cells[:, cols - LANES:], lane_at, 1)
         go_left[tile] = jnp.where((lane >= lane_at) & (lane < lane_at + width), head, go_left[tile])
         go_right[tile] = jnp.where((lane >= lane_at - width) & (lane < lane_at), tail, go_right[tile])
 
-    def every_field(act):
-        for m in range(members):
-            tile, base = m // PER_TILE, (m % PER_TILE) * MEMBER_LANES
-            act(guess_ext.at[m, 0], lambda: ice * guess_ref[m, 0], guess_at[2 * m], GUESS_W, tile, base + U_AT)
-            act(guess_ext.at[m, 1], lambda: ice * guess_ref[m, 1], guess_at[2 * m + 1], GUESS_W, tile, base + V_AT)
+    def every_field(act, group):
+        if group == 0:
+            act(thick_ext, lambda: ice * thick_ref[...], flat_at[0], FLAT_W, 0, 0, FLAT_AT)
+            act(surf_ext, lambda: surf_ref[...], flat_at[1], FLAT_W, 0, 1, FLAT_AT)
+        for k in range(PER_TILE):
+            m, base = group * PER_TILE + k, k * MEMBER_LANES
+            act(guess_ext.at[m, 0], lambda: ice * guess_ref[m, 0], guess_at[2 * k], GUESS_W, group, group, base + U_AT)
+            act(guess_ext.at[m, 1], lambda: ice * guess_ref[m, 1], guess_at[2 * k + 1], GUESS_W, group, group, base + V_AT)
             act(drag_ext.at[m], lambda: ice * (ground * fric_ref[m].astype(F32) + water_drag),
-                drag_at[m], DRAG_W, tile, base + DRAG_AT)
-        act(thick_ext, lambda: ice * thick_ref[...], flat_at[0], FLAT_W, 0, FLAT_AT)
-        act(surf_ext, lambda: surf_ref[...], flat_at[1], FLAT_W, 1, FLAT_AT)
-
-    every_field(lambda ext, cells, *where: pack(ext, cells(), *where))
+                drag_at[k], DRAG_W, group, group, base + DRAG_AT)
+
+    for group in range(2):
+        every_field(lambda ext, cells, *where: pack(ext, cells(), *where), group)
 
     pl.semaphore_wait(barrier, len(greeted))
     above, mid, below = pl.ds(0, EDGE), pl.ds(EDGE, rows), pl.ds(EDGE + rows, EDGE)
     first, final = pl.ds(0, EDGE), pl.ds(rows - EDGE, EDGE)
+    late = pl.ds(0, pl.cdiv(flat_at[0], EDGE) * EDGE)
     moves = [
-        (go_up, in_down),
-        (go_down, in_up),
-        (go_left, in_right.at[:, mid]),
-        (go_right, in_left.at[:, mid]),
-        (go_left.at[:, first], in_right.at[:, below]),
-        (go_right.at[:, first], in_left.at[:, below]),
-        (go_left.at[:, final], in_right.at[:, above]),
-        (go_right.at[:, final], in_left.at[:, above]),
+        (0, go_up.at[0], in_down.at[0]),
+        (1, go_down.at[0], in_up.at[0]),
+        (2, go_left, in_right.at[:, mid]),
+        (3, go_right, in_left.at[:, mid]),
+        (4, go_left.at[:, first], in_right.at[:, below]),
+        (5, go_right.at[:, first], in_left.at[:, below]),
+        (6, go_left.at[:, final], in_right.at[:, above]),
+        (7, go_right.at[:, final], in_left.at[:, above]),
+        (0, go_up.at[1, late], in_down.at[1, late]),
+        (1, go_down.at[1, late], in_up.at[1, late]),
     ]
     copies = [
         pltpu.make_async_remote_copy(
             src_ref=source, dst_ref=target, send_sem=send_sem.at[i], recv_sem=recv_sem.at[i],
-            device_id=around[i], device_id_type=MESH)
-        for i, (source, target) in enumerate(moves)
+            device_id=around[place], device_id_type=MESH)
+        for i, (place, source, target) in enumerate(moves)
     ]
     for copy in copies:
         copy.start()
-    for copy in copies:
+    batches = copies[:len(around)], copies[len(around):]
+    for copy in batches[0]:
         copy.wait_recv()
 
     row = lax.broadcasted_iota(jnp.int32, (high, LANES), 0)
@@ -177,14 +180,14 @@
         east = jnp.where(is_right, 0.0, in_right[tile])
         strip[tile] = jnp.where(outside, 0.0, west + east)
 
-    def fill(ext, cells, row_at, width, tile, lane_at):
+    def fill(ext, cells, row_at, width, group, tile, lane_at):
         for t in range(TILES):
             part = slice(t * LANES, (t + 1) * LANES)
-            ext[t, EDGE - width:EDGE, :] = jnp.where(is_top, 0.0, in_up[row_at:row_at + width, part])
-            ext[t, EDGE + rows:EDGE + rows + width, :] = jnp.where(is_low, 0.0, in_down[row_at:row_at + width, part])
+            ext[t, EDGE - width:EDGE, :] = jnp.where(is_top, 0.0, in_up[group, row_at:row_at + width, part])
+            ext[t, EDGE + rows:EDGE + rows + width, :] = jnp.where(is_low, 0.0, in_down[group, row_at:row_at + width, part])
         ext[TILES] = shift(strip[tile], -lane_at, 1)
 
-    every_field(fill)
+    every_field(fill, 0)
 
     zero = me_x // lax.axis_size("gx")
     window, start = rows + 2 * HALF, EDGE - HALF + zero
@@ -227,7 +230,7 @@
     own_row = lax.broadcasted_iota(jnp.int32, (window, LANES), 0)
     own_row = (own_row >= HALF) & (own_row < HALF + rows)
 
-    def member(m, line):
+    def member(m, carry):
         thick = tiles_of(thick_ext)
         drag = tiles_of(drag_ext.at[m])
         u, v, a, b, c = strains(guess_ext.at[m, 0], guess_ext.at[m, 1])
@@ -269,14 +272,21 @@
         def dot(fu, fv, gu, gv):
             return [jnp.where(own_row, fu[t] * gu[t] + fv[t] * gv[t], 0.0) for t in range(TILES)]
 
-        slot = lax.broadcasted_iota(jnp.int32, (1, LANES), 1)
         for i, cells in enumerate((dot(res_u, res_v, z_u, z_v), dot(res_u, res_v, y_u, y_v),
                                    dot(gap_u, gap_v, y_u, y_v), energy)):
-            total = jnp.sum(sum(cells[1:], cells[0]), axis=(0, 1), keepdims=True)
-            line = jnp.where(slot == i * QUARTER + m, total, line)
-        return line
-
-    total = lax.fori_loop(0, members, member, jnp.zeros((1, LANES), F32), unroll=4)
+            sums_ref[pl.ds(i * members + m, 1), :] = jnp.sum(sum(cells[1:], cells[0]), axis=0, keepdims=True)
+        return carry
+
+    for group in range(2):
+        if group:
+            for copy in batches[group]:
+                copy.wait_recv()
+            every_field(fill, group)
+        lax.fori_loop(group * PER_TILE, (group + 1) * PER_TILE, member, 0, unroll=PER_TILE)
+    sums = jnp.sum(sums_ref[...], axis=1, keepdims=True)
+    slot = lax.broadcasted_iota(jnp.int32, (sums.shape[0], LANES), 0) == lax.broadcasted_iota(
+        jnp.int32, (sums.shape[0], LANES), 1)
+    total = jnp.sum(jnp.where(slot, sums, 0.0), axis=0, keepdims=True)
 
     pushes = []
     for phase, (size, me, others) in enumerate(phases):
@@ -297,7 +307,7 @@
             total = total + slots[i]
         pushes += batch
 
-    rz, cross, square, energy = (shift(total, -i * QUARTER, 1) for i in range(4))
+    rz, cross, square, energy = (shift(total, -i * members, 1) for i in range(4))
     scale = rz + cross
     alpha = rz / scale
     mixed = cross + square
@@ -320,12 +330,13 @@
 def per_device(velocity_guess, friction, thickness, surface, ice_mask, grounded_mask):
     members, _, rows, cols = velocity_guess.shape
     fields = (velocity_guess, friction, thickness, surface, ice_mask, grounded_mask)
-    packed = row_places(members)[3]
+    packed = row_places()[2][1] + FLAT_W
+    packed = pl.cdiv(packed, EDGE) * EDGE
     high = rows + 2 * EDGE
     flat = (TILES + 1, high, LANES)
     count_x, count_y = lax.axis_size("gx"), lax.axis_size("gy")
     most = max(count_x, count_y)
-    line, block, side = (packed, cols), (2, rows, LANES), (2, high, LANES)
+    line, block, side = (2, packed, cols), (2, rows, LANES), (2, high, LANES)
     field = (members, 2, rows, cols)
     return pl.pallas_call(
         kernel,
@@ -336,8 +347,8 @@
         + [pltpu.VMEM(shape, F32) for shape in (
             line, line, block, block, line, line, side, side,
             (members, 2) + flat, (members,) + flat, flat, flat, side,
-            (members, 2) + flat, (members, 2) + flat, flat, flat, flat, flat, flat, (2, most, 1, LANES))]
-        + [pltpu.SemaphoreType.DMA((6,)), pltpu.SemaphoreType.DMA((8,)), pltpu.SemaphoreType.DMA((8,)),
+            (members, 2) + flat, (members, 2) + flat, flat, flat, flat, flat, flat, (4 * members, LANES), (2, most, 1, LANES))]
+        + [pltpu.SemaphoreType.DMA((6,)), pltpu.SemaphoreType.DMA((10,)), pltpu.SemaphoreType.DMA((10,)),
            pltpu.SemaphoreType.DMA((2, most)), pltpu.SemaphoreType.DMA((2,))],
         compiler_params=pltpu.CompilerParams(
             collective_id=0, has_side_effects=True, vmem_limit_bytes=60 << 20),

time: 40.7 us -> 39.5 us (0.971)
  Pallas kernels: 38.7 us -> 37.4 us
    pallas_call x1, Pallas kernels: 38.7 us -> 37.4 us  [per_device(): pl.pallas_call(kernel, out_shape=jax.ShapeDtypeStruct(field, F32), in_spe...]
where the time goes in v4:
time: 39.5 us; the launch traced here: 39.3 us
  Pallas kernels  37.4 us (95%)
  local copies, waits for them, and re-layouts  1.88 us (5%)
    pallas_call x1, Pallas kernels, per_device(): pl.pallas_call(kernel, out_shape=jax.ShapeDtypeStruct(field, F32), in_spe...  37.4 us
    unnamed x1, local copies, waits for them, and re-layouts  1.88 us

profile of v4, /device:TPU:1, one launch (start us, length us, event | category | flops | bytes accessed | tf_op | source)
XLA Modules:
  0.0 39.3 jit_solution(6936773855824785106)
XLA Ops:
  0.0 37.4 %ice.1 = f32[8,2,32,256]{3,2,1,0:T(8,128)} custom-call(f32[8,2,32,256]{3,2,1,0:T(8,128)} %guess_hbm.1, bf16[8,32,256]{2,1,0:T(8,128)(2,1)} %fric_hbm.1, f32[32,256]{1,0:T(8,128)} %thick_hbm.1, f32[32,256]{1,0:T(8,128)} %surf_hbm.1, s32[32,256]{1,0:T(8,128)} %ice_hbm.1, s32[32,256]{1,0:T(8,128)} %ground_hbm.1), custom_call_target="tpu_custom_call" | custom-call | tf_op jit(solution)/shard_map/ice/pallas_call | solution.py:341
  37.4 1.9 %copy.8 = f32[8,2,32,256]{3,2,1,0:T(8,128)} copy(f32[8,2,32,256]{3,2,1,0:T(8,128)} %ice.1) | data formatting | bytes 1048576

commit v5 on v4

--- a/solution.py
+++ b/solution.py
@@ -77,11 +77,12 @@
     fine = 4 if rows % 4 == 0 else 1
     pair = 2 if cols % 2 == 0 else 1
     me_x, me_y = lax.axis_index("gx"), lax.axis_index("gy")
-    place_y, others_y = spread([(cols // pair, me_y // pair, 1.0), (pair, lax.rem(me_y, pair), 0.1)])
-    place_x, others_x = spread([(rows // fine, me_x // fine, 1.0), (fine, lax.rem(me_x, fine), 1.0)])
+    wide, deep, tall, core = lax.rem(me_x, fine), me_x // fine, me_y // pair, lax.rem(me_y, pair)
+    place_z, others_z = spread([(rows // fine, deep, 1.0), (pair, core, 0.1)])
+    place_y, others_y = spread([(cols // pair, tall, 1.0), (fine, wide, 1.0)])
     return [
-        (cols, place_y, [(me_x, chip * pair + core) for chip, core in others_y]),
-        (rows, place_x, [(deep * fine + wide, me_y) for deep, wide in others_x]),
+        (rows // fine * pair, place_z, [(d * fine + wide, tall * pair + c) for d, c in others_z]),
+        (cols // pair * fine, place_y, [(deep * fine + w, t * pair + core) for t, w in others_y]),
     ]
 
 
@@ -288,24 +289,26 @@
         jnp.int32, (sums.shape[0], LANES), 1)
     total = jnp.sum(jnp.where(slot, sums, 0.0), axis=0, keepdims=True)
 
-    pushes = []
     for phase, (size, me, others) in enumerate(phases):
         slots = held.at[phase]
         slots[me] = total
         batch = [
             pltpu.make_async_remote_copy(
-                src_ref=slots.at[me], dst_ref=slots.at[me], send_sem=push_sem.at[phase, i],
+                src_ref=slots.at[me], dst_ref=slots.at[me], send_sem=push_sem.at[phase],
                 recv_sem=pull_sem.at[phase], device_id=place, device_id_type=MESH)
-            for i, place in enumerate(others)
+            for place in others
         ]
         for push in batch:
             push.start()
         everything = slots.at[pl.ds(0, size - 1)]
+        if phase == 0:
+            for copy in copies:
+                copy.wait_send()
+        pltpu.make_async_copy(everything, everything, push_sem.at[phase]).wait()
         pltpu.make_async_copy(everything, everything, pull_sem.at[phase]).wait()
         total = slots[0]
         for i in range(1, size):
             total = total + slots[i]
-        pushes += batch
 
     rz, cross, square, energy = (shift(total, -i * members, 1) for i in range(4))
     scale = rz + cross
@@ -323,8 +326,6 @@
                 own = pl.ds(EDGE, rows)
                 out_ref[m, i, :, t * LANES:(t + 1) * LANES] = guess_ext[m, i, t, own, :] + (
                     by_z * z_ref[m, i, t, own, :] + by_y * y_ref[m, i, t, own, :])
-    for copy in copies + pushes:
-        copy.wait_send()
 
 
 def per_device(velocity_guess, friction, thickness, surface, ice_mask, grounded_mask):
@@ -349,7 +350,7 @@
             (members, 2) + flat, (members,) + flat, flat, flat, side,
             (members, 2) + flat, (members, 2) + flat, flat, flat, flat, flat, flat, (4 * members, LANES), (2, most, 1, LANES))]
         + [pltpu.SemaphoreType.DMA((6,)), pltpu.SemaphoreType.DMA((10,)), pltpu.SemaphoreType.DMA((10,)),
-           pltpu.SemaphoreType.DMA((2, most)), pltpu.SemaphoreType.DMA((2,))],
+           pltpu.SemaphoreType.DMA((2,)), pltpu.SemaphoreType.DMA((2,))],
         compiler_params=pltpu.CompilerParams(
             collective_id=0, has_side_effects=True, vmem_limit_bytes=60 << 20),
         name="ice",

time: 39.5 us -> 38.6 us (0.977)
  Pallas kernels: 37.4 us -> 36.6 us
    pallas_call x1, Pallas kernels: 37.4 us -> 36.6 us  [per_device(): pl.pallas_call(kernel, out_shape=jax.ShapeDtypeStruct(field, F32), in_spe...]
where the time goes in v5:
time: 38.6 us; the launch traced here: 38.5 us
  Pallas kernels  36.6 us (95%)
  local copies, waits for them, and re-layouts  1.88 us (5%)
    pallas_call x1, Pallas kernels, per_device(): pl.pallas_call(kernel, out_shape=jax.ShapeDtypeStruct(field, F32), in_spe...  36.6 us
    unnamed x1, local copies, waits for them, and re-layouts  1.88 us

profile of v5, /device:TPU:1, one launch (start us, length us, event | category | flops | bytes accessed | tf_op | source)
XLA Modules:
  0.0 38.5 jit_solution(16675249177511457214)
XLA Ops:
  0.0 36.6 %ice.1 = f32[8,2,32,256]{3,2,1,0:T(8,128)} custom-call(f32[8,2,32,256]{3,2,1,0:T(8,128)} %guess_hbm.1, bf16[8,32,256]{2,1,0:T(8,128)(2,1)} %fric_hbm.1, f32[32,256]{1,0:T(8,128)} %thick_hbm.1, f32[32,256]{1,0:T(8,128)} %surf_hbm.1, s32[32,256]{1,0:T(8,128)} %ice_hbm.1, s32[32,256]{1,0:T(8,128)} %ground_hbm.1), custom_call_target="tpu_custom_call" | custom-call | tf_op jit(solution)/shard_map/ice/pallas_call | solution.py:342
  36.6 1.9 %copy.8 = f32[8,2,32,256]{3,2,1,0:T(8,128)} copy(f32[8,2,32,256]{3,2,1,0:T(8,128)} %ice.1) | data formatting | bytes 1048576

commit v6 on v5

--- a/solution.py
+++ b/solution.py
@@ -18,6 +18,7 @@
 MEMBER_LANES = 2 * (GUESS_W + GUESS_W + DRAG_W)
 U_AT, V_AT, DRAG_AT = GUESS_W, 3 * GUESS_W, 4 * GUESS_W + DRAG_W
 PER_TILE = 4
+EARLY = 3
 FLAT_AT = PER_TILE * MEMBER_LANES + FLAT_W
 EDGE, HALF = 8, 4
 LANES, TILES = 128, 2
@@ -51,11 +52,15 @@
     return a * (a + b) + b * b + c * (0.25 * c)
 
 
-def row_places():
-    guess = [GUESS_W * i for i in range(2 * PER_TILE)]
-    drag = [GUESS_W * 2 * PER_TILE + DRAG_W * i for i in range(PER_TILE)]
-    flat = GUESS_W * 2 * PER_TILE + DRAG_W * PER_TILE
-    return guess, drag, (flat, flat + FLAT_W)
+def row_places(count):
+    guess = [GUESS_W * i for i in range(2 * count)]
+    drag = [GUESS_W * 2 * count + DRAG_W * i for i in range(count)]
+    flat = GUESS_W * 2 * count + DRAG_W * count
+    return guess, drag, (flat, flat + FLAT_W), flat + 2 * FLAT_W
+
+
+def whole_rows(count):
+    return pl.cdiv(count, EDGE) * EDGE
 
 
 def spread(axes):
@@ -100,19 +105,19 @@
     targets = (ice_ref, ground_ref, thick_ref, surf_ref, guess_ref, fric_ref)
     loads = [pltpu.make_async_copy(source, target, load_sem.at[i])
              for i, (source, target) in enumerate(zip(sources, targets))]
-    for load in loads:
-        load.start()
-
     barrier = pltpu.get_barrier_semaphore()
     greeted = [place for _, _, others in phases[::-1] for place in others] + around
     for place in greeted:
         pl.semaphore_signal(barrier, inc=1, device_id=place, device_id_type=MESH)
+    for load in loads:
+        load.start()
 
     members, _, rows, cols = guess_ref.shape
     high = rows + 2 * EDGE
     is_top, is_low = me_x == 0, me_x == lax.axis_size("gx") - 1
     is_left, is_right = me_y == 0, me_y == lax.axis_size("gy") - 1
-    guess_at, drag_at, flat_at = row_places()
+    batch_of = (range(0, EARLY), range(EARLY, members))
+    placed = [row_places(len(batch)) for batch in batch_of]
 
     go_left[...] = jnp.zeros_like(go_left)
     go_right[...] = jnp.zeros_like(go_right)
@@ -134,14 +139,15 @@
 
     def every_field(act, group):
         if group == 0:
-            act(thick_ext, lambda: ice * thick_ref[...], flat_at[0], FLAT_W, 0, 0, FLAT_AT)
-            act(surf_ext, lambda: surf_ref[...], flat_at[1], FLAT_W, 0, 1, FLAT_AT)
-        for k in range(PER_TILE):
-            m, base = group * PER_TILE + k, k * MEMBER_LANES
-            act(guess_ext.at[m, 0], lambda: ice * guess_ref[m, 0], guess_at[2 * k], GUESS_W, group, group, base + U_AT)
-            act(guess_ext.at[m, 1], lambda: ice * guess_ref[m, 1], guess_at[2 * k + 1], GUESS_W, group, group, base + V_AT)
+            act(thick_ext, lambda: ice * thick_ref[...], placed[0][2][0], FLAT_W, 0, 0, FLAT_AT)
+            act(surf_ext, lambda: surf_ref[...], placed[0][2][1], FLAT_W, 0, 1, FLAT_AT)
+        guess_at, drag_at = placed[group][:2]
+        for k, m in enumerate(batch_of[group]):
+            tile, base = m // PER_TILE, (m % PER_TILE) * MEMBER_LANES
+            act(guess_ext.at[m, 0], lambda: ice * guess_ref[m, 0], guess_at[2 * k], GUESS_W, group, tile, base + U_AT)
+            act(guess_ext.at[m, 1], lambda: ice * guess_ref[m, 1], guess_at[2 * k + 1], GUESS_W, group, tile, base + V_AT)
             act(drag_ext.at[m], lambda: ice * (ground * fric_ref[m].astype(F32) + water_drag),
-                drag_at[k], DRAG_W, group, group, base + DRAG_AT)
+                drag_at[k], DRAG_W, group, tile, base + DRAG_AT)
 
     for group in range(2):
         every_field(lambda ext, cells, *where: pack(ext, cells(), *where), group)
@@ -149,10 +155,10 @@
     pl.semaphore_wait(barrier, len(greeted))
     above, mid, below = pl.ds(0, EDGE), pl.ds(EDGE, rows), pl.ds(EDGE + rows, EDGE)
     first, final = pl.ds(0, EDGE), pl.ds(rows - EDGE, EDGE)
-    late = pl.ds(0, pl.cdiv(flat_at[0], EDGE) * EDGE)
+    early, late = pl.ds(0, whole_rows(placed[0][3])), pl.ds(0, whole_rows(placed[1][2][0]))
     moves = [
-        (0, go_up.at[0], in_down.at[0]),
-        (1, go_down.at[0], in_up.at[0]),
+        (0, go_up.at[0, early], in_down.at[0, early]),
+        (1, go_down.at[0, early], in_up.at[0, early]),
         (2, go_left, in_right.at[:, mid]),
         (3, go_right, in_left.at[:, mid]),
         (4, go_left.at[:, first], in_right.at[:, below]),
@@ -283,7 +289,8 @@
             for copy in batches[group]:
                 copy.wait_recv()
             every_field(fill, group)
-        lax.fori_loop(group * PER_TILE, (group + 1) * PER_TILE, member, 0, unroll=PER_TILE)
+        batch = batch_of[group]
+        lax.fori_loop(batch.start, batch.stop, member, 0, unroll=len(batch))
     sums = jnp.sum(sums_ref[...], axis=1, keepdims=True)
     slot = lax.broadcasted_iota(jnp.int32, (sums.shape[0], LANES), 0) == lax.broadcasted_iota(
         jnp.int32, (sums.shape[0], LANES), 1)
@@ -331,8 +338,7 @@
 def per_device(velocity_guess, friction, thickness, surface, ice_mask, grounded_mask):
     members, _, rows, cols = velocity_guess.shape
     fields = (velocity_guess, friction, thickness, surface, ice_mask, grounded_mask)
-    packed = row_places()[2][1] + FLAT_W
-    packed = pl.cdiv(packed, EDGE) * EDGE
+    packed = whole_rows(max(row_places(EARLY)[3], row_places(members - EARLY)[2][0]))
     high = rows + 2 * EDGE
     flat = (TILES + 1, high, LANES)
     count_x, count_y = lax.axis_size("gx"), lax.axis_size("gy")

time: 38.6 us -> 38.7 us (level)
  no operation moved by 1% of the time
where the time goes in v6:
time: 38.7 us; the launch traced here: 38.5 us
  Pallas kernels  36.6 us (95%)
  local copies, waits for them, and re-layouts  1.88 us (5%)
    pallas_call x1, Pallas kernels, per_device(): pl.pallas_call(kernel, out_shape=jax.ShapeDtypeStruct(field, F32), in_spe...  36.6 us
    unnamed x1, local copies, waits for them, and re-layouts  1.88 us

profile of v6, /device:TPU:1, one launch (start us, length us, event | category | flops | bytes accessed | tf_op | source)
XLA Modules:
  0.0 38.5 jit_solution(4354662334473383473)
XLA Ops:
  0.0 36.6 %ice.1 = f32[8,2,32,256]{3,2,1,0:T(8,128)} custom-call(f32[8,2,32,256]{3,2,1,0:T(8,128)} %guess_hbm.1, bf16[8,32,256]{2,1,0:T(8,128)(2,1)} %fric_hbm.1, f32[32,256]{1,0:T(8,128)} %thick_hbm.1, f32[32,256]{1,0:T(8,128)} %surf_hbm.1, s32[32,256]{1,0:T(8,128)} %ice_hbm.1, s32[32,256]{1,0:T(8,128)} %ground_hbm.1), custom_call_target="tpu_custom_call" | custom-call | tf_op jit(solution)/shard_map/ice/pallas_call | solution.py:348
  36.6 1.9 %copy.8 = f32[8,2,32,256]{3,2,1,0:T(8,128)} copy(f32[8,2,32,256]{3,2,1,0:T(8,128)} %ice.1) | data formatting | bytes 1048576
